TPU v7x, 128 devices: a whole 4x4x4 slice. The times are simulated.
128 devices in a mesh: seq: 16 (over x, y), cand: 8 (over z, core).
Axes of the slice: x: 4, y: 4, z: 4, core: 2. Of those that a mesh axis runs over, the one named last changes fastest.
Arguments:
- behaviors: float32 [8, 131072, 128], P('cand', 'seq'), may hold values from -15 to 15
- cluster_ids: int32 [8, 131072], P('cand', 'seq'), may hold values from 0 to 2047, as said below
- lengths: int32 [8, 16], P('cand', 'seq'), may hold values from 2048 to 8192
- candidates: bfloat16 [8, 4096, 128], P(None, ('seq', 'cand')), may hold values from -6 to 6
- w_query: bfloat16 [128, 128], replicated, may hold values from -0.5 to 0.5
- w_key: bfloat16 [128, 128], replicated, may hold values from -0.5 to 0.5
- w_hidden: bfloat16 [256, 512], replicated, may hold values from -0.375 to 0.375
- b_hidden: float32 [512], replicated, may hold values from -0.5 to 0.5
- w_out: float32 [512], replicated, may hold values from -0.25 to 0.25
Outputs:
- ranking: float32 [8, 4096], P(None, ('seq', 'cand'))
Inputs may be any that keep to these rules, and one draw needn't show every extreme that they name: `cluster_ids`: each user's first 2048 slots name 2048 different clusters.
All inputs are finite; a program needn't handle non-finite values.
Results may differ from a plain program's by a relative error of at most 0.02.
Values may be sent and summed in bfloat16 or wider, within the bound.
A program may use at most 64 MiB of HBM per device.

v0:
```python
import jax
import jax.numpy as jnp
from jax import lax
from jax.sharding import PartitionSpec as P

C = 2048


def cluster_partials(item_rows, cluster_ids, length):
    slots = item_rows.shape[0]
    block_rows = min(512, slots)
    labels = jnp.arange(C, dtype=jnp.int32)

    def accumulate(carry, number):
        totals, tallies = carry
        offset = number * block_rows
        piece = lax.dynamic_slice_in_dim(item_rows, offset, block_rows, 0)
        idents = lax.dynamic_slice_in_dim(cluster_ids, offset, block_rows, 0)
        inside = offset + jnp.arange(block_rows, dtype=jnp.int32) < length
        onehot = ((idents[:, None] == labels[None, :]) & inside[:, None]).astype(jnp.bfloat16)
        upper = lax.optimization_barrier(piece.astype(jnp.bfloat16))
        lower = (piece - upper.astype(jnp.float32)).astype(jnp.bfloat16)
        dims = (((0,), (0,)), ((), ()))
        totals = totals + lax.dot_general(onehot, upper, dims, preferred_element_type=jnp.float32)
        totals = totals + lax.dot_general(onehot, lower, dims, preferred_element_type=jnp.float32)
        tallies = tallies + jnp.sum(onehot, axis=0, dtype=jnp.float32)
        return ((totals, tallies), None)

    start = (jnp.zeros((C, item_rows.shape[1]), jnp.float32), jnp.zeros((C,), jnp.float32))
    (totals, tallies), _ = lax.scan(
        accumulate, start, jnp.arange(slots // block_rows, dtype=jnp.int32)
    )
    return (totals, tallies)


def statistics(sums, counts):
    centroids = (sums / jnp.maximum(counts, 1.0)[..., None]).astype(jnp.bfloat16)
    size_bias = jnp.where(counts > 0, jnp.log(1.0 + counts), jnp.float32(-1000000000.0)).astype(
        jnp.bfloat16
    )
    return (centroids, size_bias)


def make_keys(centroids, w_key):
    return jnp.einsum("ukd,de->uke", centroids, w_key, preferred_element_type=jnp.float32).astype(
        jnp.bfloat16
    )


def rank_rows(candidates, key_rows, centroids, size_bias, w_query, w_hidden, b_hidden, w_out):
    users, local_cands, width = candidates.shape
    queries = jnp.dot(
        candidates.reshape(users * local_cands, width), w_query, preferred_element_type=jnp.float32
    )
    queries = queries.astype(jnp.bfloat16).reshape(users, local_cands, width)
    scores = jnp.einsum(
        "ucd,ukd->uck", queries, key_rows, preferred_element_type=jnp.float32
    ) / jnp.sqrt(jnp.float32(width))
    scores = scores + size_bias.astype(jnp.float32)[:, None, :]
    weights = jax.nn.softmax(scores, axis=-1).astype(jnp.bfloat16)
    attended = jnp.einsum(
        "uck,ukd->ucd", weights, centroids, preferred_element_type=jnp.float32
    ).astype(jnp.bfloat16)
    features = jnp.concatenate([candidates, attended], axis=-1).reshape(
        users * local_cands, 2 * width
    )
    hidden = jax.nn.relu(jnp.dot(features, w_hidden, preferred_element_type=jnp.float32) + b_hidden)
    ranking = jnp.dot(hidden, w_out, precision=lax.Precision.HIGHEST)
    return ranking.reshape(users, local_cands)


def on_device(
    behaviors, cluster_ids, lengths, candidates, w_query, w_key, w_hidden, b_hidden, w_out
):
    partials, counts = jax.vmap(cluster_partials)(behaviors, cluster_ids, lengths[:, 0])
    sums, tallies = (
        lax.psum(partials.astype(jnp.bfloat16), "seq").astype(jnp.float32),
        lax.psum(counts.astype(jnp.bfloat16), "seq").astype(jnp.float32),
    )
    centroids, size_bias = statistics(sums, tallies)
    key_rows = make_keys(centroids, w_key)
    mine = lax.all_to_all(candidates, "cand", split_axis=0, concat_axis=1, tiled=True)
    scored = rank_rows(mine, key_rows, centroids, size_bias, w_query, w_hidden, b_hidden, w_out)
    return lax.all_to_all(scored, "cand", split_axis=1, concat_axis=0, tiled=True)


def solution(mesh):
    in_specs = (
        P("cand", "seq", None),
        P("cand", "seq"),
        P("cand", "seq"),
        P(None, ("seq", "cand"), None),
        P(),
        P(),
        P(),
        P(),
        P(),
    )
    out_specs = P(None, ("seq", "cand"))
    return jax.shard_map(
        on_device, mesh=mesh, in_specs=in_specs, out_specs=out_specs, check_vma=False
    )
```

profile of v0, /device:TPU:1, one launch (start us, length us, event | category | flops | bytes accessed | tf_op | source)
XLA Modules:
  0.0 258.1 jit_solution(13973427605766248245)
XLA Ops:
  6.5 6.9 %all-to-all-start = ((bf16[8,32,128]{2,1,0:T(8,128)(2,1)}), bf16[8,32,128]{2,1,0:T(8,128)(2,1)S(1)}, u32[]{:S(2)}, u32[]{:S(2)}) async-start(bf16[8,32,128]{2,1,0:T(8,128)(2,1)} %param.14), calls=%async_computation | async-start | bytes 131072 | tf_op jit(solution)/shard_map/all_to_all | solution.py:82
  13.5 135.2 %while.16 = (s32[]{:T(128)}, f32[1,2048,128]{2,1,0:T(8,128)S(1)}, f32[1,2048]{1,0:T(1,128)S(1)}, s32[16]{0:T(128)S(1)}, s32[1,8192]{1,0:T(1,128)}, /*index=5*/s3...) while((s32[]{:T(128)}, f32[1,2048,128]{2,1,0:T(8,128)S(1)}, ...), condition=%wide.region_2.3_spmd.clone.clone, body=%wide.region_0.2_spmd.clone.clone.sunk | while | flops 547294208 | bytes 5026022 | solution.py:30
  17.0 1.0 dynamic-slice_convert_fusion.2
  18.0 1.5 fusion.66
  19.5 2.5 fusion.67
  25.4 1.0 dynamic-slice_convert_fusion.2
  26.4 1.5 fusion.66
  27.9 2.5 fusion.67
  34.9 1.5 fusion.66
  36.4 2.5 fusion.67
  43.3 1.5 fusion.66
  44.8 2.5 fusion.67
  50.8 1.0 dynamic-slice_convert_fusion.2
  51.8 1.5 fusion.66
  53.3 2.5 fusion.67
  59.2 1.0 dynamic-slice_convert_fusion.2
  60.3 1.5 fusion.66
  61.7 2.5 fusion.67
  67.7 1.0 dynamic-slice_convert_fusion.2
  68.7 1.5 fusion.66
  70.2 2.5 fusion.67
  76.1 1.0 dynamic-slice_convert_fusion.2
  77.2 1.5 fusion.66
  78.6 2.5 fusion.67
  85.6 1.5 fusion.66
  87.1 2.5 fusion.67
  94.1 1.5 fusion.66
  95.5 2.5 fusion.67
  101.5 1.0 dynamic-slice_convert_fusion.2
  102.5 1.5 fusion.66
  104.0 2.5 fusion.67
  109.9 1.0 dynamic-slice_convert_fusion.2
  111.0 1.5 fusion.66
  112.4 2.5 fusion.67
  118.4 1.0 dynamic-slice_convert_fusion.2
  119.4 1.5 fusion.66
  120.9 2.5 fusion.67
  126.8 1.0 dynamic-slice_convert_fusion.2
  127.9 1.5 fusion.66
  129.4 2.5 fusion.67
  136.3 1.5 fusion.66
  137.8 2.5 fusion.67
  144.8 1.5 fusion.66
  146.3 2.5 fusion.67
  149.7 34.1 %psum.15 = bf16[1,2048]{1,0:T(2,128)(2,1)S(1)} all-reduce(bf16[1,2048]{1,0:T(2,128)(2,1)S(1)} %convert_element_type.78), channel_id=1, replica_groups=mesh['seq'=16,'cand'=8] {'seq'}, use_global_device_ids=true, to_apply=%region_4.5 | all-reduce | flops 2048 | bytes 8192 | tf_op jit(solution)/shard_map/psum | solution.py:78
  184.1 50.4 %all-reduce.2.cloned.1.call-done = bf16[1,2048,128]{2,1,0:T(8,128)(2,1)} async-done(((bf16[1,2048,128]{2,1,0:T(8,128)(2,1)}), bf16[1,2048,128]{2,1,0:T(8,128)(2,1)}) %all-reduce.2.cloned.1.call-update) | async-done | bytes 524304 | tf_op jit(solution)/shard_map/psum | solution.py:77
  234.4 1.9 fusion.44
  239.2 11.5 %all_to_all.28 = f32[1,8,32]{2,0,1:T(1,128)S(1)} all-to-all(f32[1,8,32]{2,0,1:T(1,128)S(1)} %all_to_all.23), channel_id=1, replica_groups=mesh['seq'=16,'cand'=8] {'cand'}, dimensions={1} | all-to-all | bytes 2048 | tf_op jit(solution)/shard_map/all_to_all | solution.py:84
  (131 shorter events, 56.8 us)
Async XLA Ops:
  6.5 231.8 %copy-start = (bf16[256,512]{1,0:T(8,128)(2,1)S(1)}, bf16[256,512]{1,0:T(8,128)(2,1)}, u32[]{:S(2)}) copy-start(bf16[256,512]{1,0:T(8,128)(2,1)} %param.17) | copy-start | bytes 786436
  6.5 177.2 %all-to-all-start = ((bf16[8,32,128]{2,1,0:T(8,128)(2,1)}), bf16[8,32,128]{2,1,0:T(8,128)(2,1)S(1)}, u32[]{:S(2)}, u32[]{:S(2)}) async-start(bf16[8,32,128]{2,1,0:T(8,128)(2,1)} %param.14), calls=%async_computation | async-start | bytes 131072 | tf_op jit(solution)/shard_map/all_to_all | solution.py:82
  13.5 221.0 %all-reduce.2.cloned.1.call-start = ((), (), s32[]{:S(2)}) async-start(), calls=%async_computation.2 | async-start | bytes 1048576 | tf_op jit(solution)/shard_map/psum | solution.py:77
  148.7 35.2 %copy-start.1 = (bf16[128,128]{1,0:T(8,128)(2,1)S(1)}, bf16[128,128]{1,0:T(8,128)(2,1)}, u32[]{:S(2)}) copy-start(bf16[128,128]{1,0:T(8,128)(2,1)} %param.15) | copy-start | bytes 98308
  148.7 85.7 %copy-start.5 = (bf16[128,128]{1,0:T(8,128)(2,1)S(1)}, bf16[128,128]{1,0:T(8,128)(2,1)}, u32[]{:S(2)}) copy-start(bf16[128,128]{1,0:T(8,128)(2,1)} %param.16) | copy-start | bytes 98308
  236.3 1.0 copy-start.4
  237.4 1.0 copy-start.2
  237.4 1.2 copy-start.3
Sparse Core Ops, SparseCore 0:
  149.8 84.6 all-reduce.1
where the time goes:
time: 260 us; the launch traced here: 258 us
  matrix products  66.7 us (26%)
  waiting for transfers between devices  50.4 us (19%)
  blocking collectives  45.5 us (18%)
  local copies, waits for them, and re-layouts  38 us (15%)
  other arithmetic  27.1 us (10%)
  between operations  13.5 us (5%)
  loops' own time  9.9 us (4%)
  starting transfers between devices  6.94 us (3%)
    psum x1, waiting for transfers between devices, on_device(): lax.psum(partials.astype(jnp.bfloat16), 'seq').astype(jnp.float32)  50.4 us
    dot_general x16, matrix products, accumulate(): lax.dot_general(onehot, lower, dims, preferred_element_type=jnp.float32)  39.4 us
    psum x1, blocking collectives, on_device(): lax.psum(counts.astype(jnp.bfloat16), 'seq').astype(jnp.float32)  34.1 us
    dot_general x16, matrix products, accumulate(): lax.dot_general(onehot, upper, dims, preferred_element_type=jnp.float32)  23.6 us
    convert_element_type x16, local copies, waits for them, and re-layouts, accumulate(): upper = lax.optimization_barrier(piece.astype(jnp.bfloat16))  16.4 us
    reduce_sum x16, other arithmetic, accumulate(): tallies = tallies + jnp.sum(onehot, axis=0, dtype=jnp.float32)  13.8 us
    all_to_all x1, blocking collectives, on_device(): lax.all_to_all(scored, 'cand', split_axis=1, concat_axis=0, tiled=True)  11.5 us
    while x16, local copies, waits for them, and re-layouts, accumulate(): idents = lax.dynamic_slice_in_dim(cluster_ids, offset, block_rows, 0)  10.9 us
  transfers between devices with their start and end apart: 2, of which 1 were waited for; matrix products, arithmetic and copies ran while one was open for 49% of the time, Pallas kernels for 0%

commit v1 on v0

v1 whole, which is shorter than its diff:
```python
import jax
import jax.numpy as jnp
from jax import lax
from jax.experimental import pallas as pl
from jax.experimental.pallas import tpu as pltpu
from jax.sharding import PartitionSpec as P

BF16 = jnp.bfloat16
F32 = jnp.float32
NX, NY, NCAND = 4, 4, 8
SLOTS, D, HID = 8192, 128, 512
HALF = 1024
CHUNKS = 4
CH = SLOTS // CHUNKS
MB = 256
ROWS = HALF // 16


def remote(src, dst, send, recv, device_id):
    return pltpu.make_async_remote_copy(
        src_ref=src,
        dst_ref=dst,
        send_sem=send,
        recv_sem=recv,
        device_id=device_id,
        device_id_type=pl.DeviceIdType.MESH,
    )


def nt_dot(a, b):
    return lax.dot_general(a, b, (((1,), (1,)), ((), ())), preferred_element_type=F32)


def kernel(
    len_ref,
    beh_ref,
    ids_ref,
    ids2_ref,
    cand_ref,
    wq_ref,
    wk_ref,
    wh_ref,
    bh_ref,
    wo_ref,
    out_ref,
    beh_v,
    rhs,
    rowid,
    acc,
    own,
    s_send,
    rs_buf,
    cnt_send,
    cnt_buf,
    ga,
    gb,
    mine,
    q2,
    wt,
    hc,
    bcol,
    wcol,
    out_send,
    out_buf,
    sc,
    load_sem,
    cand_s,
    cand_r,
    cnt_s,
    cnt_r,
    rs_s,
    rs_r,
    ag_s,
    ag_r,
    out_s,
    out_r,
):
    s = lax.axis_index("seq")
    c = lax.axis_index("cand")
    x, y = s // NY, s % NY

    loads = [
        pltpu.make_async_copy(
            beh_ref.at[0, pl.ds(k * CH, CH), :], beh_v.at[pl.ds(k * CH, CH), :], load_sem.at[k]
        )
        for k in range(CHUNKS)
    ]
    for cp in loads:
        cp.start()

    def seq_at(dx, dy):
        return ((x + dx) % NX) * NY + (y + dy) % NY

    barrier = pltpu.get_barrier_semaphore()
    for k in range(1, 16):
        pl.semaphore_signal(
            barrier, inc=1, device_id=(seq_at(k // 4, k % 4), c), device_id_type=pl.DeviceIdType.MESH
        )
    for j in range(1, NCAND):
        pl.semaphore_signal(
            barrier, inc=1, device_id=(s, (c + j) % NCAND), device_id_type=pl.DeviceIdType.MESH
        )

    length = len_ref[0, 0]
    idrow = ids_ref[...]
    live = lax.broadcasted_iota(jnp.int32, (1, SLOTS), 1) < length
    rowid[...] = jnp.where(live, idrow & (HALF - 1), 4096).astype(F32)
    ahot_row = jnp.where(live, idrow >> 7, 4096).astype(F32)
    ids_t = jnp.concatenate([ids2_ref[...], ids2_ref[...]], axis=0).T

    pl.semaphore_wait(barrier, 22)

    cand_copies = []
    for j in range(1, NCAND):
        peer = (c + j) % NCAND
        cp = remote(cand_ref.at[peer], mine.at[c], cand_s.at[j], cand_r.at[j], (s, peer))
        cp.start()
        cand_copies.append(cp)
    mine[c] = cand_ref[c]

    iota16 = lax.broadcasted_iota(jnp.int32, (MB, 128), 0).astype(F32).astype(BF16)

    def onehot(r0, k0, kc):
        rel = rowid[:, pl.ds(k0, kc)] - r0
        b16 = jnp.broadcast_to(rel, (16, kc)).astype(BF16)
        cols = []
        for t in range(kc // 128):
            bb = jnp.broadcast_to(b16[None, :, t * 128 : (t + 1) * 128], (MB // 16, 16, 128))
            cols.append(jnp.where(iota16 == bb.reshape(MB, 128), BF16(1), BF16(0)))
        return jnp.concatenate(cols, axis=1)

    def block_start(i):
        return (((x + 1 + i) % NX) * MB).astype(F32)

    lane = lax.broadcasted_iota(jnp.int32, (128, 128), 1)
    a_iota = lax.broadcasted_iota(jnp.int32, (16, CH), 0).astype(F32)
    counts = jnp.zeros((16, 128), F32)
    for k in range(CHUNKS):
        loads[k].wait()
        bh = []
        for g in range(k * (CH // 128), (k + 1) * (CH // 128)):
            col = jnp.broadcast_to(ids_t[:, g : g + 1], (128, 128))
            v = beh_v[g * 128 : (g + 1) * 128, :]
            upper = col >= HALF
            rhs[g * 128 : (g + 1) * 128, :128] = jnp.where(upper, 0.0, v).astype(BF16)
            rhs[g * 128 : (g + 1) * 128, 128:] = jnp.where(upper, v, 0.0).astype(BF16)
            bh.append(jnp.where((col & 127) == lane, 1.0, 0.0).astype(BF16))
        ah = jnp.where(
            jnp.broadcast_to(ahot_row[:, k * CH : (k + 1) * CH], (16, CH)) == a_iota, 1.0, 0.0
        ).astype(BF16)
        counts = counts + jnp.dot(ah, jnp.concatenate(bh, axis=0), preferred_element_type=F32)
        part = jnp.dot(
            onehot(block_start(0), k * CH, CH),
            rhs[k * CH : (k + 1) * CH, :],
            preferred_element_type=F32,
        )
        if k == 0:
            acc[...] = part
        else:
            acc[...] += part
    s_send[0] = acc[...].astype(BF16)
    cnt_send[...] = counts

    def rs_copy(i, dy):
        k = ((1 + i) % 4) * 4 + dy
        peer_y = (y + dy) % NY
        return remote(
            s_send.at[i, pl.ds(pl.multiple_of(peer_y * ROWS, ROWS), ROWS), :],
            rs_buf.at[k],
            rs_s.at[k],
            rs_r.at[k],
            (((x + 1 + i) % NX) * NY + peer_y, c),
        )

    def cnt_copy(k):
        return remote(
            cnt_send, cnt_buf.at[k], cnt_s.at[k], cnt_r.at[k], (seq_at(k // 4, k % 4), c)
        )

    for dy in range(4):
        rs_copy(0, dy).start()
    for k in range(1, 16):
        cnt_copy(k).start()

    for cp in cand_copies:
        cp.wait()
    cands = mine[...].reshape(256, 128)
    q = jnp.dot(cands, wq_ref[...], preferred_element_type=F32).astype(BF16)
    q2[...] = nt_dot(q, wk_ref[...]).astype(BF16)
    wt[...] = wh_ref[...].astype(F32).T.astype(BF16)
    bcol[...] = jnp.broadcast_to(bh_ref[...], (128, HID)).T
    wcol[...] = jnp.broadcast_to(wo_ref[...], (128, HID)).T
    hc[...] = nt_dot(wt[:, :D], cands) + jnp.concatenate([bcol[...], bcol[...]], axis=1)

    def block(i):
        return jnp.dot(
            onehot(block_start(i), 0, SLOTS), rhs[...], preferred_element_type=F32
        )

    for i in range(1, 4):
        val = block(i)
        s_send[i] = val.astype(BF16)
        if i < 3:
            for dy in range(4):
                rs_copy(i, dy).start()
        else:
            own[...] = val
            for dy in range(1, 4):
                rs_copy(i, dy).start()

    total = own[pl.ds(pl.multiple_of(y * ROWS, ROWS), ROWS), :]
    for i in range(4):
        for dy in range(4):
            k = ((1 + i) % 4) * 4 + dy
            if k:
                rs_copy(i, dy).wait()
                total = total + rs_buf[k].astype(F32)
    tb = total.astype(BF16)

    def at_rows(ref, px, py):
        return ref.at[pl.ds(pl.multiple_of((px * NY + py) * ROWS, ROWS), ROWS), :]

    at_rows(ga, x, y)[...] = tb[:, :128]
    at_rows(gb, x, y)[...] = tb[:, 128:]

    def ag1(half, d):
        if half == 0:
            blk = at_rows(ga, x, y)
            dev = ((x + d) % NX) * NY + y
        else:
            blk = at_rows(gb, x, y)
            dev = x * NY + (y + d) % NY
        n = half * 16 + d
        return remote(blk, blk, ag_s.at[n], ag_r.at[n], (dev, c))

    def ag2(half, d, e):
        if half == 0:
            blk = at_rows(ga, (x + NX - d) % NX, y)
            dev = x * NY + (y + e) % NY
        else:
            blk = at_rows(gb, x, (y + NY - d) % NY)
            dev = ((x + e) % NX) * NY + y
        n = half * 16 + 4 + d * 3 + e - 1
        return remote(blk, blk, ag_s.at[n], ag_r.at[n], (dev, c))

    order = (1, 3, 2)
    for d in order:
        for half in range(2):
            ag1(half, d).start()
    for d in order:
        for half in range(2):
            ag2(half, 0, d).start()

    for k in range(1, 16):
        cnt_copy(k).wait()
    tot = cnt_send[...]
    for k in range(1, 16):
        tot = tot + cnt_buf[k]
    inv = 1.0 / jnp.maximum(tot, 1.0)
    mult = inv * (1.0 / jnp.sqrt(F32(D)))
    bias = jnp.where(tot > 0, jnp.log(1.0 + tot), F32(-1e9)).astype(BF16).astype(F32)

    for d in order:
        for half in range(2):
            ag1(half, d).wait()
            for e in order:
                ag2(half, d, e).start()
    for d in (0,) + order:
        for half in range(2):
            for e in order:
                ag2(half, d, e).wait()

    gs = (ga, gb)
    mx = jnp.full((256, 128), -jnp.inf, F32)
    for h in range(2):
        raw = nt_dot(q2[...], gs[h][...])
        for j in range(8):
            r = h * 8 + j
            t = raw[:, j * 128 : (j + 1) * 128] * mult[r : r + 1, :] + bias[r : r + 1, :]
            sc[:, r * 128 : (r + 1) * 128] = t
            mx = jnp.maximum(mx, t)
    mx = jnp.broadcast_to(jnp.max(mx, axis=1, keepdims=True), (256, 128))
    den = jnp.zeros((256, 128), F32)
    att = jnp.zeros((256, 128), F32)
    for h in range(2):
        ps = []
        for j in range(8):
            r = h * 8 + j
            e = jnp.exp(sc[:, r * 128 : (r + 1) * 128] - mx)
            den = den + e
            ps.append((e * inv[r : r + 1, :]).astype(BF16))
        att = att + jnp.dot(
            jnp.concatenate(ps, axis=1), gs[h][...], preferred_element_type=F32
        )
    att = (att / jnp.sum(den, axis=1, keepdims=True)).astype(BF16)

    hid = jnp.maximum(hc[...] + nt_dot(wt[:, D:], att), 0.0)
    hid = hid * jnp.concatenate([wcol[...], wcol[...]], axis=1)
    row = jnp.sum(hid, axis=0, keepdims=True)
    for j in range(NCAND):
        out_send[j, :, :32] = row[:, j * 32 : (j + 1) * 32]
    back = []
    for j in range(1, NCAND):
        peer = (c + j) % NCAND
        cp = remote(out_send.at[peer], out_buf.at[c], out_s.at[j], out_r.at[j], (s, peer))
        cp.start()
        back.append(cp)
    out_buf[c] = out_send[c]
    for cp in back:
        cp.wait()
    out_ref[...] = out_buf[:, 0, :32]


def on_device(
    behaviors, cluster_ids, lengths, candidates, w_query, w_key, w_hidden, b_hidden, w_out
):
    vmem = pl.BlockSpec(memory_space=pltpu.VMEM)
    dma = pltpu.SemaphoreType.DMA
    return pl.pallas_call(
        kernel,
        out_shape=jax.ShapeDtypeStruct((8, 32), F32),
        in_specs=[
            pl.BlockSpec(memory_space=pltpu.SMEM),
            pl.BlockSpec(memory_space=pl.ANY),
        ]
        + [vmem] * 8,
        out_specs=vmem,
        scratch_shapes=[
            pltpu.VMEM((SLOTS, D), F32),
            pltpu.VMEM((SLOTS, 2 * D), BF16),
            pltpu.VMEM((1, SLOTS), F32),
            pltpu.VMEM((MB, 2 * D), F32),
            pltpu.VMEM((MB, 2 * D), F32),
            pltpu.VMEM((4, MB, 2 * D), BF16),
            pltpu.VMEM((16, ROWS, 2 * D), BF16),
            pltpu.VMEM((16, 128), F32),
            pltpu.VMEM((16, 16, 128), F32),
            pltpu.VMEM((HALF, D), BF16),
            pltpu.VMEM((HALF, D), BF16),
            pltpu.VMEM((8, 32, D), BF16),
            pltpu.VMEM((256, D), BF16),
            pltpu.VMEM((HID, 2 * D), BF16),
            pltpu.VMEM((HID, 256), F32),
            pltpu.VMEM((HID, 128), F32),
            pltpu.VMEM((HID, 128), F32),
            pltpu.VMEM((8, 1, 128), F32),
            pltpu.VMEM((8, 1, 128), F32),
            pltpu.VMEM((256, 2048), F32),
            dma((CHUNKS,)),
            dma((8,)),
            dma((8,)),
            dma((16,)),
            dma((16,)),
            dma((16,)),
            dma((16,)),
            dma((32,)),
            dma((32,)),
            dma((8,)),
            dma((8,)),
        ],
        compiler_params=pltpu.CompilerParams(collective_id=0, has_side_effects=True),
        name="fused",
    )(
        lengths,
        behaviors,
        cluster_ids,
        cluster_ids.reshape(64, 128),
        candidates,
        w_query,
        w_key,
        w_hidden,
        b_hidden.reshape(1, HID),
        w_out.reshape(1, HID),
    )


def solution(mesh):
    in_specs = (
        P("cand", "seq", None),
        P("cand", "seq"),
        P("cand", "seq"),
        P(None, ("seq", "cand"), None),
        P(),
        P(),
        P(),
        P(),
        P(),
    )
    return jax.shard_map(
        on_device,
        mesh=mesh,
        in_specs=in_specs,
        out_specs=P(None, ("seq", "cand")),
        check_vma=False,
    )
```

time: 260 us -> 42.9 us (0.17)
  matrix products: 66.7 us -> 0 us
  waiting for transfers between devices: 50.4 us -> 0 us
  blocking collectives: 45.5 us -> 0 us
  Pallas kernels: 0 us -> 40.8 us
  local copies, waits for them, and re-layouts: 38 us -> 1.28 us
  other arithmetic: 27.1 us -> 0 us
  between operations: 13.5 us -> 0.66 us
  loops' own time: 9.9 us -> 0 us
  starting transfers between devices: 6.94 us -> 0 us
    dot_general x37 -> x0, matrix products: 66.7 us -> none  [the longest x16 39.4 us: accumulate(): lax.dot_general(onehot, lower, dims, preferred_element_type=jnp.float32)]
    psum x1 -> x0, waiting for transfers between devices: 50.4 us -> none  [on_device(): lax.psum(partials.astype(jnp.bfloat16), 'seq').astype(jnp.float32)]
    pallas_call x0 -> x1, Pallas kernels: none -> 40.8 us  [on_device(): pl.pallas_call(kernel, out_shape=jax.ShapeDtypeStruct((8, 32), F32), in_s...]
    psum x1 -> x0, blocking collectives: 34.1 us -> none  [on_device(): lax.psum(counts.astype(jnp.bfloat16), 'seq').astype(jnp.float32)]
    convert_element_type x16 -> x0, local copies, waits for them, and re-layouts: 16.4 us -> none  [accumulate(): upper = lax.optimization_barrier(piece.astype(jnp.bfloat16))]
    reduce_sum x17 -> x0, other arithmetic: 14.2 us -> none  [the longest x16 13.8 us: accumulate(): tallies = tallies + jnp.sum(onehot, axis=0, dtype=jnp.float32)]
    all_to_all x1 -> x0, blocking collectives: 11.5 us -> none  [on_device(): lax.all_to_all(scored, 'cand', split_axis=1, concat_axis=0, tiled=True)]
    while x16 -> x0, local copies, waits for them, and re-layouts: 10.9 us -> none  [accumulate(): idents = lax.dynamic_slice_in_dim(cluster_ids, offset, block_rows, 0)]
  transfers between devices with their start and end apart: 2 -> 0, of which waited for: 1 -> 0; matrix products, arithmetic and copies ran while one was open for 49% -> 0% of each run, Pallas kernels for 0% -> 0%
where the time goes in v1:
time: 42.9 us; the launch traced here: 42.7 us
  Pallas kernels  40.8 us (95%)
  local copies, waits for them, and re-layouts  1.28 us (3%)
  between operations  0.66 us (2%)
    pallas_call x1, Pallas kernels, on_device(): pl.pallas_call(kernel, out_shape=jax.ShapeDtypeStruct((8, 32), F32), in_s...  40.8 us
    unnamed x1, local copies, waits for them, and re-layouts  1.28 us

profile of v1, /device:TPU:1, one launch (start us, length us, event | category | flops | bytes accessed | tf_op | source)
XLA Modules:
  0.0 42.7 jit_solution(18091282104340008674)
XLA Ops:
  0.7 40.8 %fused.1 = f32[8,32]{1,0:T(8,128)} custom-call(s32[1,1]{1,0:T(1,128)S(6)} %copy.11.len_ref, f32[1,8192,128]{2,1,0:T(8,128)} %beh_ref.1, s32[1,8192]{1,0:T(1,128)} %ids_ref.1, s32[64,128]{1,0:T(8,128)} %bitcast.3, bf16[8,32,128]{2,1,0:T(8,128)(2,1)} %cand_ref.1, bf16[128,128]{1,0:T(8,128)(2,1)} %wq_ref.1, bf16[128,128]{1,0:T(8,128)(2,1)} %wk_ref.1, ...), custom_call_target="tpu_custom_call" | custom-call | tf_op jit(solution)/shard_map/fused/pallas_call | solution.py:319
  41.5 1.3 %copy.12 = f32[8,32]{1,0:T(8,128)} copy(f32[8,32]{1,0:T(8,128)} %fused.1) | data formatting | bytes 2048

commit v2 on v1

v2 whole, which is shorter than its diff:
```python
import jax
import jax.numpy as jnp
from jax import lax
from jax.experimental import pallas as pl
from jax.experimental.pallas import tpu as pltpu
from jax.sharding import PartitionSpec as P

BF16 = jnp.bfloat16
F32 = jnp.float32
NX, NY, NCAND = 4, 4, 8
SLOTS, D, HID = 8192, 128, 512
HALF = 1024
CHUNKS = 4
CH = SLOTS // CHUNKS
MB = 256
ROWS = HALF // 16


def remote(src, dst, send, recv, device_id):
    return pltpu.make_async_remote_copy(
        src_ref=src,
        dst_ref=dst,
        send_sem=send,
        recv_sem=recv,
        device_id=device_id,
        device_id_type=pl.DeviceIdType.MESH,
    )


def nt_dot(a, b):
    return lax.dot_general(a, b, (((1,), (1,)), ((), ())), preferred_element_type=F32)


SETS = (
    ((2, 2), (1, 2), (3, 2), (2, 3)),
    ((1, 3), (3, 3), (0, 2), (2, 1)),
    ((0, 3), (1, 1), (3, 1), (2, 0)),
    ((0, 0), (1, 0), (3, 0), (0, 1)),
)
ORDER = (1, 3, 2)


def kernel(
    len_hbm,
    beh_hbm,
    ids_hbm,
    ids2_hbm,
    cand_hbm,
    wq_hbm,
    wk_hbm,
    wh_hbm,
    bh_hbm,
    wo_hbm,
    out_ref,
    len_ref,
    beh_v,
    ids_ref,
    ids2_ref,
    cand_ref,
    wq_ref,
    wk_ref,
    wh_ref,
    bh_ref,
    wo_ref,
    rhs,
    rowid,
    acc,
    own,
    s_send,
    rs_buf,
    cnt_x,
    cnt_xb,
    cnt_y,
    cnt_yb,
    ga,
    gb,
    mine,
    q2,
    wt,
    hc,
    bcol,
    wcol,
    out_send,
    out_buf,
    sc,
    load_sem,
    op_sem,
    cand_s,
    cand_r,
    cnt_s,
    cnt_r,
    rs_s,
    rs_r,
    ag_s,
    ag_r,
    out_s,
    out_r,
):
    s = lax.axis_index("seq")
    c = lax.axis_index("cand")
    x, y = s // NY, s % NY

    pairs = (
        (len_hbm, len_ref),
        (ids_hbm, ids_ref),
        (ids2_hbm, ids2_ref),
        (cand_hbm, cand_ref),
        (wq_hbm, wq_ref),
        (wk_hbm, wk_ref),
        (wh_hbm, wh_ref),
        (bh_hbm, bh_ref),
        (wo_hbm, wo_ref),
    )
    ops = [pltpu.make_async_copy(a, b, op_sem.at[n]) for n, (a, b) in enumerate(pairs)]
    loads = [
        pltpu.make_async_copy(
            beh_hbm.at[0, pl.ds(k * CH, CH), :], beh_v.at[pl.ds(k * CH, CH), :], load_sem.at[k]
        )
        for k in range(CHUNKS)
    ]
    for cp in ops[:3] + loads + ops[3:]:
        cp.start()

    def seq_at(dx, dy):
        return ((x + dx) % NX) * NY + (y + dy) % NY

    barrier = pltpu.get_barrier_semaphore()
    for k in range(1, 16):
        pl.semaphore_signal(
            barrier, inc=1, device_id=(seq_at(k // 4, k % 4), c), device_id_type=pl.DeviceIdType.MESH
        )
    for j in range(1, NCAND):
        pl.semaphore_signal(
            barrier, inc=1, device_id=(s, (c + j) % NCAND), device_id_type=pl.DeviceIdType.MESH
        )

    for cp in ops[:3]:
        cp.wait()
    length = len_ref[0, 0]
    idrow = ids_ref[...]
    live = lax.broadcasted_iota(jnp.int32, (1, SLOTS), 1) < length
    rowid[...] = jnp.where(live, idrow & (HALF - 1), 4096).astype(F32)
    ahot_row = jnp.where(live, idrow >> 7, 4096).astype(F32)
    ids_t = jnp.concatenate([ids2_ref[...], ids2_ref[...]], axis=0).T
    half_t = (ids_t >> 10).astype(F32).astype(BF16)
    low_t = (ids_t & 127).astype(F32).astype(BF16)

    iota16 = lax.broadcasted_iota(jnp.int32, (ROWS, 128), 0).astype(F32).astype(BF16)

    def onehot(i, k0, kc):
        parts = []
        for dx, dy in SETS[i]:
            rel = rowid[:, pl.ds(k0, kc)] - (seq_at(dx, dy) * ROWS).astype(F32)
            b16 = jnp.broadcast_to(rel, (16, kc)).astype(BF16)
            cols = []
            for t in range(kc // 128):
                bb = jnp.broadcast_to(b16[None, :, t * 128 : (t + 1) * 128], (ROWS // 16, 16, 128))
                cols.append(jnp.where(iota16 == bb.reshape(ROWS, 128), BF16(1), BF16(0)))
            parts.append(jnp.concatenate(cols, axis=1))
        return jnp.concatenate(parts, axis=0)

    lane = lax.broadcasted_iota(jnp.int32, (128, 128), 1).astype(F32).astype(BF16)
    a_iota = lax.broadcasted_iota(jnp.int32, (16, CH), 0).astype(F32).astype(BF16)
    zero = BF16(0)
    counts = jnp.zeros((16, 128), F32)
    for k in range(CHUNKS):
        loads[k].wait()
        bh = []
        for g in range(k * (CH // 128), (k + 1) * (CH // 128)):
            upper = jnp.broadcast_to(half_t[:, g : g + 1], (128, 128)) != zero
            v = beh_v[g * 128 : (g + 1) * 128, :].astype(BF16)
            rhs[g * 128 : (g + 1) * 128, :128] = jnp.where(upper, zero, v)
            rhs[g * 128 : (g + 1) * 128, 128:] = jnp.where(upper, v, zero)
            low = jnp.broadcast_to(low_t[:, g : g + 1], (128, 128))
            bh.append(jnp.where(low == lane, BF16(1), zero))
        ab = jnp.broadcast_to(ahot_row[:, k * CH : (k + 1) * CH], (16, CH)).astype(BF16)
        ah = jnp.where(ab == a_iota, BF16(1), zero)
        counts = counts + jnp.dot(ah, jnp.concatenate(bh, axis=0), preferred_element_type=F32)
        part = jnp.dot(
            onehot(0, k * CH, CH), rhs[k * CH : (k + 1) * CH, :], preferred_element_type=F32
        )
        if k == 0:
            acc[...] = part
        else:
            acc[...] += part
    s_send[0] = acc[...].astype(BF16)
    cnt_x[...] = counts

    def rs_copy(i, j):
        dx, dy = SETS[i][j]
        k = dx * 4 + dy
        return remote(
            s_send.at[i, pl.ds(j * ROWS, ROWS), :],
            rs_buf.at[k],
            rs_s.at[k],
            rs_r.at[k],
            (seq_at(dx, dy), c),
        )

    def cntx_copy(d):
        return remote(cnt_x, cnt_xb.at[d], cnt_s.at[d], cnt_r.at[d], (seq_at(d, 0), c))

    def cnty_copy(d):
        return remote(cnt_y, cnt_yb.at[d], cnt_s.at[4 + d], cnt_r.at[4 + d], (seq_at(0, d), c))

    ops[3].wait()
    pl.semaphore_wait(barrier, 22)
    for j in range(4):
        rs_copy(0, j).start()
    for d in ORDER:
        cntx_copy(d).start()
    cand_copies = []
    for j in range(1, NCAND):
        peer = (c + j) % NCAND
        cp = remote(cand_ref.at[peer], mine.at[c], cand_s.at[j], cand_r.at[j], (s, peer))
        cp.start()
        cand_copies.append(cp)
    mine[c] = cand_ref[c]

    for i in range(1, 4):
        val = jnp.dot(onehot(i, 0, SLOTS), rhs[...], preferred_element_type=F32)
        s_send[i] = val.astype(BF16)
        if i == 2:
            for d in ORDER:
                cntx_copy(d).wait()
            cnt_y[...] = cnt_x[...] + cnt_xb[1] + cnt_xb[2] + cnt_xb[3]
        if i == 3:
            own[...] = val[:ROWS]
        for j in range(4):
            if SETS[i][j] != (0, 0):
                rs_copy(i, j).start()
        if i == 2:
            for d in ORDER:
                cnty_copy(d).start()

    for cp in ops[4:]:
        cp.wait()
    for cp in cand_copies:
        cp.wait()
    cands = mine[...].reshape(256, 128)
    q = jnp.dot(cands, wq_ref[...], preferred_element_type=F32).astype(BF16)
    q2[...] = nt_dot(q, wk_ref[...]).astype(BF16)
    wt[...] = wh_ref[...].astype(F32).T.astype(BF16)
    bcol[...] = jnp.broadcast_to(bh_ref[...], (128, HID)).T
    wcol[...] = jnp.broadcast_to(wo_ref[...], (128, HID)).T
    hc[...] = nt_dot(wt[:, :D], cands) + jnp.concatenate([bcol[...], bcol[...]], axis=1)
    for d in ORDER:
        cnty_copy(d).wait()
    tot = cnt_y[...] + cnt_yb[1] + cnt_yb[2] + cnt_yb[3]
    inv = 1.0 / jnp.maximum(tot, 1.0)
    mult = inv * (1.0 / jnp.sqrt(F32(D)))
    bias = jnp.where(tot > 0, jnp.log(1.0 + tot), F32(-1e9)).astype(BF16).astype(F32)

    total = own[...]
    for i in range(4):
        for j in range(4):
            dx, dy = SETS[i][j]
            if (dx, dy) != (0, 0):
                rs_copy(i, j).wait()
                total = total + rs_buf[dx * 4 + dy].astype(F32)
    tb = total.astype(BF16)

    def at_rows(ref, px, py):
        return ref.at[pl.ds(pl.multiple_of((px * NY + py) * ROWS, ROWS), ROWS), :]

    at_rows(ga, x, y)[...] = tb[:, :128]
    at_rows(gb, x, y)[...] = tb[:, 128:]

    def ag1(half, d):
        blk = at_rows((ga, gb)[half], x, y)
        dev = seq_at(d, 0) if half == 0 else seq_at(0, d)
        n = half * 16 + d
        return remote(blk, blk, ag_s.at[n], ag_r.at[n], (dev, c))

    def ag2(half, d, e):
        n = half * 16 + 4 + d * 3 + e - 1
        if (d, e) == (2, 2):
            blk = at_rows((ga, gb)[half], x, y)
            dev = seq_at(2, 2)
        elif half == 0:
            blk = at_rows(ga, (x + NX - d) % NX, y)
            dev = seq_at(0, e)
        else:
            blk = at_rows(gb, x, (y + NY - d) % NY)
            dev = seq_at(e, 0)
        return remote(blk, blk, ag_s.at[n], ag_r.at[n], (dev, c))

    for d in ORDER:
        for half in range(2):
            ag1(half, d).start()
    for half in range(2):
        ag2(half, 2, 2).start()
    for d in (2, 1, 3):
        for half in range(2):
            ag2(half, 0, d).start()
    for d in ORDER:
        for half in range(2):
            ag1(half, d).wait()
            for e in (2, 1, 3):
                if (d, e) != (2, 2):
                    ag2(half, d, e).start()
    for d in (0,) + ORDER:
        for half in range(2):
            for e in ORDER:
                ag2(half, d, e).wait()

    gs = (ga, gb)
    mx = jnp.full((256, 128), -jnp.inf, F32)
    for h in range(2):
        raw = nt_dot(q2[...], gs[h][...])
        for j in range(8):
            r = h * 8 + j
            t = raw[:, j * 128 : (j + 1) * 128] * mult[r : r + 1, :] + bias[r : r + 1, :]
            sc[:, r * 128 : (r + 1) * 128] = t
            mx = jnp.maximum(mx, t)
    mx = jnp.broadcast_to(jnp.max(mx, axis=1, keepdims=True), (256, 128))
    den = jnp.zeros((256, 128), F32)
    att = jnp.zeros((256, 128), F32)
    for h in range(2):
        ps = []
        for j in range(8):
            r = h * 8 + j
            e = jnp.exp(sc[:, r * 128 : (r + 1) * 128] - mx)
            den = den + e
            ps.append((e * inv[r : r + 1, :]).astype(BF16))
        att = att + jnp.dot(
            jnp.concatenate(ps, axis=1), gs[h][...], preferred_element_type=F32
        )
    att = (att / jnp.sum(den, axis=1, keepdims=True)).astype(BF16)

    hid = jnp.maximum(hc[...] + nt_dot(wt[:, D:], att), 0.0)
    hid = hid * jnp.concatenate([wcol[...], wcol[...]], axis=1)
    row = jnp.sum(hid, axis=0, keepdims=True)
    for j in range(NCAND):
        out_send[j, :, :32] = row[:, j * 32 : (j + 1) * 32]
    back = []
    for j in range(1, NCAND):
        peer = (c + j) % NCAND
        cp = remote(out_send.at[peer], out_buf.at[c], out_s.at[j], out_r.at[j], (s, peer))
        cp.start()
        back.append(cp)
    out_buf[c] = out_send[c]
    for cp in back:
        cp.wait()
    out_ref[...] = out_buf[:, 0, :32]


def on_device(
    behaviors, cluster_ids, lengths, candidates, w_query, w_key, w_hidden, b_hidden, w_out
):
    vmem = pl.BlockSpec(memory_space=pltpu.VMEM)
    dma = pltpu.SemaphoreType.DMA
    return pl.pallas_call(
        kernel,
        out_shape=jax.ShapeDtypeStruct((8, 32), F32),
        in_specs=[pl.BlockSpec(memory_space=pltpu.HBM)] * 10,
        out_specs=vmem,
        scratch_shapes=[
            pltpu.SMEM((1, 1), jnp.int32),
            pltpu.VMEM((SLOTS, D), F32),
            pltpu.VMEM((1, SLOTS), jnp.int32),
            pltpu.VMEM((64, 128), jnp.int32),
            pltpu.VMEM((8, 32, D), BF16),
            pltpu.VMEM((D, D), BF16),
            pltpu.VMEM((D, D), BF16),
            pltpu.VMEM((2 * D, HID), BF16),
            pltpu.VMEM((1, HID), F32),
            pltpu.VMEM((1, HID), F32),
            pltpu.VMEM((SLOTS, 2 * D), BF16),
            pltpu.VMEM((1, SLOTS), F32),
            pltpu.VMEM((MB, 2 * D), F32),
            pltpu.VMEM((ROWS, 2 * D), F32),
            pltpu.VMEM((4, MB, 2 * D), BF16),
            pltpu.VMEM((16, ROWS, 2 * D), BF16),
            pltpu.VMEM((16, 128), F32),
            pltpu.VMEM((4, 16, 128), F32),
            pltpu.VMEM((16, 128), F32),
            pltpu.VMEM((4, 16, 128), F32),
            pltpu.VMEM((HALF, D), BF16),
            pltpu.VMEM((HALF, D), BF16),
            pltpu.VMEM((8, 32, D), BF16),
            pltpu.VMEM((256, D), BF16),
            pltpu.VMEM((HID, 2 * D), BF16),
            pltpu.VMEM((HID, 256), F32),
            pltpu.VMEM((HID, 128), F32),
            pltpu.VMEM((HID, 128), F32),
            pltpu.VMEM((8, 1, 128), F32),
            pltpu.VMEM((8, 1, 128), F32),
            pltpu.VMEM((256, 2048), F32),
            dma((CHUNKS,)),
            dma((9,)),
            dma((8,)),
            dma((8,)),
            dma((8,)),
            dma((8,)),
            dma((16,)),
            dma((16,)),
            dma((32,)),
            dma((32,)),
            dma((8,)),
            dma((8,)),
        ],
        compiler_params=pltpu.CompilerParams(collective_id=0, has_side_effects=True),
        name="fused",
    )(
        lengths,
        behaviors,
        cluster_ids,
        cluster_ids.reshape(64, 128),
        candidates,
        w_query,
        w_key,
        w_hidden,
        b_hidden.reshape(1, HID),
        w_out.reshape(1, HID),
    )


def solution(mesh):
    in_specs = (
        P("cand", "seq", None),
        P("cand", "seq"),
        P("cand", "seq"),
        P(None, ("seq", "cand"), None),
        P(),
        P(),
        P(),
        P(),
        P(),
    )
    return jax.shard_map(
        on_device,
        mesh=mesh,
        in_specs=in_specs,
        out_specs=P(None, ("seq", "cand")),
        check_vma=False,
    )
```

time: 42.9 us -> 37.5 us (0.87)
  Pallas kernels: 40.8 us -> 35.5 us
    pallas_call x1, Pallas kernels: 40.8 us -> 35.5 us  [on_device(): pl.pallas_call(kernel, out_shape=jax.ShapeDtypeStruct((8, 32), F32), in_s...]
where the time goes in v2:
time: 37.5 us; the launch traced here: 37.4 us
  Pallas kernels  35.5 us (95%)
  local copies, waits for them, and re-layouts  1.28 us (3%)
  between operations  0.66 us (2%)
    pallas_call x1, Pallas kernels, on_device(): pl.pallas_call(kernel, out_shape=jax.ShapeDtypeStruct((8, 32), F32), in_s...  35.5 us
    unnamed x1, local copies, waits for them, and re-layouts  1.28 us

profile of v2, /device:TPU:1, one launch (start us, length us, event | category | flops | bytes accessed | tf_op | source)
XLA Modules:
  0.0 37.4 jit_solution(9819997301355080360)
XLA Ops:
  0.7 35.5 %fused.1 = f32[8,32]{1,0:T(8,128)} custom-call(s32[1,1]{1,0:T(1,128)S(6)} %copy.11.len_hbm, f32[1,8192,128]{2,1,0:T(8,128)} %beh_hbm.1, s32[1,8192]{1,0:T(1,128)} %ids_hbm.1, s32[64,128]{1,0:T(8,128)} %bitcast.3, bf16[8,32,128]{2,1,0:T(8,128)(2,1)} %cand_hbm.1, bf16[128,128]{1,0:T(8,128)(2,1)} %wq_hbm.1, bf16[128,128]{1,0:T(8,128)(2,1)} %wk_hbm.1, ...), custom_call_target="tpu_custom_call" | custom-call | tf_op jit(solution)/shard_map/fused/pallas_call | solution.py:353
  36.1 1.3 %copy.12 = f32[8,32]{1,0:T(8,128)} copy(f32[8,32]{1,0:T(8,128)} %fused.1) | data formatting | bytes 2048

commit v3 on v2

--- a/solution.py
+++ b/solution.py
@@ -63,7 +63,8 @@
     bh_ref,
     wo_ref,
     rhs,
-    rowid,
+    own16,
+    low16,
     acc,
     own,
     s_send,
@@ -82,6 +83,9 @@
     wcol,
     out_send,
     out_buf,
+    inv_ref,
+    mult_ref,
+    bias_ref,
     sc,
     load_sem,
     op_sem,
@@ -139,8 +143,13 @@
     length = len_ref[0, 0]
     idrow = ids_ref[...]
     live = lax.broadcasted_iota(jnp.int32, (1, SLOTS), 1) < length
-    rowid[...] = jnp.where(live, idrow & (HALF - 1), 4096).astype(F32)
-    ahot_row = jnp.where(live, idrow >> 7, 4096).astype(F32)
+    high = (idrow >> 8) & 3
+    mid = (idrow >> 6) & 3
+    owner_row = jnp.where(idrow >= HALF, mid * 4 + high, high * 4 + mid)
+    low_row = jnp.where(live, idrow & (ROWS - 1), 255)
+    own16[...] = jnp.broadcast_to(owner_row.astype(F32), (16, SLOTS)).astype(BF16)
+    low16[...] = jnp.broadcast_to(low_row.astype(F32), (16, SLOTS)).astype(BF16)
+    ahot_row = jnp.where(live, idrow >> 7, 255).astype(F32)
     ids_t = jnp.concatenate([ids2_ref[...], ids2_ref[...]], axis=0).T
     half_t = (ids_t >> 10).astype(F32).astype(BF16)
     low_t = (ids_t & 127).astype(F32).astype(BF16)
@@ -150,8 +159,8 @@
     def onehot(i, k0, kc):
         parts = []
         for dx, dy in SETS[i]:
-            rel = rowid[:, pl.ds(k0, kc)] - (seq_at(dx, dy) * ROWS).astype(F32)
-            b16 = jnp.broadcast_to(rel, (16, kc)).astype(BF16)
+            p16 = jnp.full((16, kc), seq_at(dx, dy).astype(F32), F32).astype(BF16)
+            b16 = jnp.where(own16[:, pl.ds(k0, kc)] == p16, low16[:, pl.ds(k0, kc)], BF16(255))
             cols = []
             for t in range(kc // 128):
                 bb = jnp.broadcast_to(b16[None, :, t * 128 : (t + 1) * 128], (ROWS // 16, 16, 128))
@@ -248,8 +257,11 @@
         cnty_copy(d).wait()
     tot = cnt_y[...] + cnt_yb[1] + cnt_yb[2] + cnt_yb[3]
     inv = 1.0 / jnp.maximum(tot, 1.0)
-    mult = inv * (1.0 / jnp.sqrt(F32(D)))
-    bias = jnp.where(tot > 0, jnp.log(1.0 + tot), F32(-1e9)).astype(BF16).astype(F32)
+    inv_ref[...] = inv
+    mult_ref[...] = inv * (1.0 / jnp.sqrt(F32(D)))
+    bias_ref[...] = (
+        jnp.where(tot > 0, jnp.log(1.0 + tot), F32(-1e9)).astype(BF16).astype(F32)
+    )
 
     total = own[...]
     for i in range(4):
@@ -260,28 +272,31 @@
                 total = total + rs_buf[dx * 4 + dy].astype(F32)
     tb = total.astype(BF16)
 
-    def at_rows(ref, px, py):
-        return ref.at[pl.ds(pl.multiple_of((px * NY + py) * ROWS, ROWS), ROWS), :]
-
-    at_rows(ga, x, y)[...] = tb[:, :128]
-    at_rows(gb, x, y)[...] = tb[:, 128:]
+    gs = (ga, gb)
+
+    def at_rows(half, px, py):
+        p = py * NX + px if half else px * NY + py
+        return gs[half].at[pl.ds(pl.multiple_of(p * ROWS, ROWS), ROWS), :]
+
+    at_rows(0, x, y)[...] = tb[:, :128]
+    at_rows(1, x, y)[...] = tb[:, 128:]
 
     def ag1(half, d):
-        blk = at_rows((ga, gb)[half], x, y)
-        dev = seq_at(d, 0) if half == 0 else seq_at(0, d)
+        blk = at_rows(half, x, y)
+        dev = seq_at(0, d) if half else seq_at(d, 0)
         n = half * 16 + d
         return remote(blk, blk, ag_s.at[n], ag_r.at[n], (dev, c))
 
     def ag2(half, d, e):
         n = half * 16 + 4 + d * 3 + e - 1
         if (d, e) == (2, 2):
-            blk = at_rows((ga, gb)[half], x, y)
+            blk = at_rows(half, x, y)
             dev = seq_at(2, 2)
         elif half == 0:
-            blk = at_rows(ga, (x + NX - d) % NX, y)
+            blk = at_rows(0, (x + NX - d) % NX, y)
             dev = seq_at(0, e)
         else:
-            blk = at_rows(gb, x, (y + NY - d) % NY)
+            blk = at_rows(1, x, (y + NY - d) % NY)
             dev = seq_at(e, 0)
         return remote(blk, blk, ag_s.at[n], ag_r.at[n], (dev, c))
 
@@ -299,33 +314,42 @@
             for e in (2, 1, 3):
                 if (d, e) != (2, 2):
                     ag2(half, d, e).start()
-    for d in (0,) + ORDER:
-        for half in range(2):
-            for e in ORDER:
-                ag2(half, d, e).wait()
-
-    gs = (ga, gb)
-    mx = jnp.full((256, 128), -jnp.inf, F32)
-    for h in range(2):
-        raw = nt_dot(q2[...], gs[h][...])
-        for j in range(8):
-            r = h * 8 + j
-            t = raw[:, j * 128 : (j + 1) * 128] * mult[r : r + 1, :] + bias[r : r + 1, :]
-            sc[:, r * 128 : (r + 1) * 128] = t
-            mx = jnp.maximum(mx, t)
-    mx = jnp.broadcast_to(jnp.max(mx, axis=1, keepdims=True), (256, 128))
-    den = jnp.zeros((256, 128), F32)
-    att = jnp.zeros((256, 128), F32)
-    for h in range(2):
-        ps = []
-        for j in range(8):
-            r = h * 8 + j
-            e = jnp.exp(sc[:, r * 128 : (r + 1) * 128] - mx)
-            den = den + e
-            ps.append((e * inv[r : r + 1, :]).astype(BF16))
-        att = att + jnp.dot(
-            jnp.concatenate(ps, axis=1), gs[h][...], preferred_element_type=F32
-        )
+
+    top = den = att = None
+    for dists in ((0,), (1, 3), (2,)):
+        keys, rows = [], []
+        for d in dists:
+            for half in range(2):
+                for e in ORDER:
+                    ag2(half, d, e).wait()
+                g = (y + NY - d) % NY if half else (x + NX - d) % NX
+                keys.append(gs[half][pl.ds(pl.multiple_of(g * MB, MB), MB), :])
+                rows += [half * 8 + g * 2, half * 8 + g * 2 + 1]
+        new = None
+        for n, kb in enumerate(keys):
+            raw = nt_dot(q2[...], kb)
+            for j in range(2):
+                r = rows[2 * n + j]
+                t = raw[:, j * 128 : (j + 1) * 128] * mult_ref[pl.ds(r, 1), :]
+                t = t + bias_ref[pl.ds(r, 1), :]
+                sc[:, (2 * n + j) * 128 : (2 * n + j + 1) * 128] = t
+                new = t if new is None else jnp.maximum(new, t)
+        new = jnp.broadcast_to(jnp.max(new, axis=1, keepdims=True), (256, 128))
+        if top is not None:
+            new = jnp.maximum(top, new)
+            alpha = jnp.exp(top - new)
+            den = den * alpha
+            att = att * alpha
+        top = new
+        for n, kb in enumerate(keys):
+            ps = []
+            for j in range(2):
+                r = rows[2 * n + j]
+                e = jnp.exp(sc[:, (2 * n + j) * 128 : (2 * n + j + 1) * 128] - top)
+                den = e if den is None else den + e
+                ps.append((e * inv_ref[pl.ds(r, 1), :]).astype(BF16))
+            pv = jnp.dot(jnp.concatenate(ps, axis=1), kb, preferred_element_type=F32)
+            att = pv if att is None else att + pv
     att = (att / jnp.sum(den, axis=1, keepdims=True)).astype(BF16)
 
     hid = jnp.maximum(hc[...] + nt_dot(wt[:, D:], att), 0.0)
@@ -352,7 +376,7 @@
     dma = pltpu.SemaphoreType.DMA
     return pl.pallas_call(
         kernel,
-        out_shape=jax.ShapeDtypeStruct((8, 32), F32),
+        out_shape=pltpu.VMEM((8, 32), F32),
         in_specs=[pl.BlockSpec(memory_space=pltpu.HBM)] * 10,
         out_specs=vmem,
         scratch_shapes=[
@@ -367,7 +391,8 @@
             pltpu.VMEM((1, HID), F32),
             pltpu.VMEM((1, HID), F32),
             pltpu.VMEM((SLOTS, 2 * D), BF16),
-            pltpu.VMEM((1, SLOTS), F32),
+            pltpu.VMEM((16, SLOTS), BF16),
+            pltpu.VMEM((16, SLOTS), BF16),
             pltpu.VMEM((MB, 2 * D), F32),
             pltpu.VMEM((ROWS, 2 * D), F32),
             pltpu.VMEM((4, MB, 2 * D), BF16),
@@ -386,7 +411,10 @@
             pltpu.VMEM((HID, 128), F32),
             pltpu.VMEM((8, 1, 128), F32),
             pltpu.VMEM((8, 1, 128), F32),
-            pltpu.VMEM((256, 2048), F32),
+            pltpu.VMEM((16, 128), F32),
+            pltpu.VMEM((16, 128), F32),
+            pltpu.VMEM((16, 128), F32),
+            pltpu.VMEM((256, 1024), F32),
             dma((CHUNKS,)),
             dma((9,)),
             dma((8,)),

time: 37.5 us -> 36.1 us (0.963)
  Pallas kernels: 35.5 us -> 34.8 us
  local copies, waits for them, and re-layouts: 1.28 us -> 0.6 us
    pallas_call x1, Pallas kernels: 35.5 us -> 34.8 us  [on_device(): pl.pallas_call(kernel, out_shape=pltpu.VMEM((8, 32), F32), in_specs=[pl.B...]
    unnamed x1, local copies, waits for them, and re-layouts: 1.28 us -> 0.6 us
where the time goes in v3:
time: 36.1 us; the launch traced here: 36 us
  Pallas kernels  34.8 us (96%)
  between operations  0.66 us (2%)
  local copies, waits for them, and re-layouts  0.6 us (2%)
    pallas_call x1, Pallas kernels, on_device(): pl.pallas_call(kernel, out_shape=pltpu.VMEM((8, 32), F32), in_specs=[pl.B...  34.8 us

profile of v3, /device:TPU:1, one launch (start us, length us, event | category | flops | bytes accessed | tf_op | source)
XLA Modules:
  0.0 36.0 jit_solution(12948089082375428524)
XLA Ops:
  0.7 34.8 %fused.1 = f32[8,32]{1,0:T(8,128)S(1)} custom-call(s32[1,1]{1,0:T(1,128)S(6)} %copy.12.len_hbm, f32[1,8192,128]{2,1,0:T(8,128)} %beh_hbm.1, s32[1,8192]{1,0:T(1,128)} %ids_hbm.1, s32[64,128]{1,0:T(8,128)} %bitcast.3, bf16[8,32,128]{2,1,0:T(8,128)(2,1)} %cand_hbm.1, bf16[128,128]{1,0:T(8,128)(2,1)} %wq_hbm.1, bf16[128,128]{1,0:T(8,128)(2,1)} %wk_hbm.1, ...), custom_call_target="tpu_custom_call" | custom-call | tf_op jit(solution)/shard_map/fused/pallas_call | solution.py:377
  35.4 0.6 %copy.11 = f32[8,32]{1,0:T(8,128)} copy(f32[8,32]{1,0:T(8,128)S(1)} %fused.1) | data formatting | bytes 2048

commit v4 on v3

--- a/solution.py
+++ b/solution.py
@@ -25,6 +25,10 @@
         device_id=device_id,
         device_id_type=pl.DeviceIdType.MESH,
     )
+
+
+def wait_bytes(ref, sem):
+    pltpu.make_async_copy(ref, ref, sem).wait()
 
 
 def nt_dot(a, b):
@@ -90,7 +94,6 @@
     load_sem,
     op_sem,
     cand_s,
-    cand_r,
     cnt_s,
     cnt_r,
     rs_s,
@@ -98,7 +101,6 @@
     ag_s,
     ag_r,
     out_s,
-    out_r,
 ):
     s = lax.axis_index("seq")
     c = lax.axis_index("cand")
@@ -156,9 +158,9 @@
 
     iota16 = lax.broadcasted_iota(jnp.int32, (ROWS, 128), 0).astype(F32).astype(BF16)
 
-    def onehot(i, k0, kc):
+    def onehot(owners, k0, kc):
         parts = []
-        for dx, dy in SETS[i]:
+        for dx, dy in owners:
             p16 = jnp.full((16, kc), seq_at(dx, dy).astype(F32), F32).astype(BF16)
             b16 = jnp.where(own16[:, pl.ds(k0, kc)] == p16, low16[:, pl.ds(k0, kc)], BF16(255))
             cols = []
@@ -167,6 +169,12 @@
                 cols.append(jnp.where(iota16 == bb.reshape(ROWS, 128), BF16(1), BF16(0)))
             parts.append(jnp.concatenate(cols, axis=1))
         return jnp.concatenate(parts, axis=0)
+
+    def block_sums(i, k0, kc):
+        return [
+            jnp.dot(onehot(owners, k0, kc), rhs[k0 : k0 + kc, :], preferred_element_type=F32)
+            for owners in (SETS[i][:2], SETS[i][2:])
+        ]
 
     lane = lax.broadcasted_iota(jnp.int32, (128, 128), 1).astype(F32).astype(BF16)
     a_iota = lax.broadcasted_iota(jnp.int32, (16, CH), 0).astype(F32).astype(BF16)
@@ -185,67 +193,54 @@
         ab = jnp.broadcast_to(ahot_row[:, k * CH : (k + 1) * CH], (16, CH)).astype(BF16)
         ah = jnp.where(ab == a_iota, BF16(1), zero)
         counts = counts + jnp.dot(ah, jnp.concatenate(bh, axis=0), preferred_element_type=F32)
-        part = jnp.dot(
-            onehot(0, k * CH, CH), rhs[k * CH : (k + 1) * CH, :], preferred_element_type=F32
-        )
-        if k == 0:
-            acc[...] = part
-        else:
-            acc[...] += part
-    s_send[0] = acc[...].astype(BF16)
+        for n, part in enumerate(block_sums(0, k * CH, CH)):
+            if k == 0:
+                acc[n] = part
+            else:
+                acc[n] += part
+    for n in range(2):
+        s_send[0, n * 2 * ROWS : (n + 1) * 2 * ROWS, :] = acc[n].astype(BF16)
     cnt_x[...] = counts
 
     def rs_copy(i, j):
-        dx, dy = SETS[i][j]
-        k = dx * 4 + dy
         return remote(
             s_send.at[i, pl.ds(j * ROWS, ROWS), :],
-            rs_buf.at[k],
-            rs_s.at[k],
-            rs_r.at[k],
-            (seq_at(dx, dy), c),
+            rs_buf.at[i * 4 + j],
+            rs_s.at[0],
+            rs_r.at[i],
+            (seq_at(*SETS[i][j]), c),
         )
 
     def cntx_copy(d):
-        return remote(cnt_x, cnt_xb.at[d], cnt_s.at[d], cnt_r.at[d], (seq_at(d, 0), c))
+        return remote(cnt_x, cnt_xb.at[d], cnt_s.at[0], cnt_r.at[0], (seq_at(d, 0), c))
 
     def cnty_copy(d):
-        return remote(cnt_y, cnt_yb.at[d], cnt_s.at[4 + d], cnt_r.at[4 + d], (seq_at(0, d), c))
+        return remote(cnt_y, cnt_yb.at[d], cnt_s.at[1], cnt_r.at[1], (seq_at(0, d), c))
 
     ops[3].wait()
     pl.semaphore_wait(barrier, 22)
+    for d in ORDER:
+        cntx_copy(d).start()
     for j in range(4):
         rs_copy(0, j).start()
-    for d in ORDER:
-        cntx_copy(d).start()
-    cand_copies = []
     for j in range(1, NCAND):
         peer = (c + j) % NCAND
-        cp = remote(cand_ref.at[peer], mine.at[c], cand_s.at[j], cand_r.at[j], (s, peer))
-        cp.start()
-        cand_copies.append(cp)
+        remote(cand_ref.at[peer], mine.at[c], cand_s.at[0], cand_s.at[1], (s, peer)).start()
     mine[c] = cand_ref[c]
 
     for i in range(1, 4):
-        val = jnp.dot(onehot(i, 0, SLOTS), rhs[...], preferred_element_type=F32)
-        s_send[i] = val.astype(BF16)
-        if i == 2:
-            for d in ORDER:
-                cntx_copy(d).wait()
-            cnt_y[...] = cnt_x[...] + cnt_xb[1] + cnt_xb[2] + cnt_xb[3]
+        val = block_sums(i, 0, SLOTS)
+        for n in range(2):
+            s_send[i, n * 2 * ROWS : (n + 1) * 2 * ROWS, :] = val[n].astype(BF16)
         if i == 3:
-            own[...] = val[:ROWS]
+            own[...] = val[0][:ROWS]
         for j in range(4):
             if SETS[i][j] != (0, 0):
                 rs_copy(i, j).start()
-        if i == 2:
-            for d in ORDER:
-                cnty_copy(d).start()
 
     for cp in ops[4:]:
         cp.wait()
-    for cp in cand_copies:
-        cp.wait()
+    wait_bytes(mine.at[pl.ds(0, 7)], cand_s.at[1])
     cands = mine[...].reshape(256, 128)
     q = jnp.dot(cands, wq_ref[...], preferred_element_type=F32).astype(BF16)
     q2[...] = nt_dot(q, wk_ref[...]).astype(BF16)
@@ -253,23 +248,15 @@
     bcol[...] = jnp.broadcast_to(bh_ref[...], (128, HID)).T
     wcol[...] = jnp.broadcast_to(wo_ref[...], (128, HID)).T
     hc[...] = nt_dot(wt[:, :D], cands) + jnp.concatenate([bcol[...], bcol[...]], axis=1)
-    for d in ORDER:
-        cnty_copy(d).wait()
-    tot = cnt_y[...] + cnt_yb[1] + cnt_yb[2] + cnt_yb[3]
-    inv = 1.0 / jnp.maximum(tot, 1.0)
-    inv_ref[...] = inv
-    mult_ref[...] = inv * (1.0 / jnp.sqrt(F32(D)))
-    bias_ref[...] = (
-        jnp.where(tot > 0, jnp.log(1.0 + tot), F32(-1e9)).astype(BF16).astype(F32)
-    )
+    wait_bytes(cnt_xb.at[pl.ds(1, 3)], cnt_r.at[0])
+    cnt_y[...] = cnt_x[...] + cnt_xb[1] + cnt_xb[2] + cnt_xb[3]
 
     total = own[...]
     for i in range(4):
-        for j in range(4):
-            dx, dy = SETS[i][j]
-            if (dx, dy) != (0, 0):
-                rs_copy(i, j).wait()
-                total = total + rs_buf[dx * 4 + dy].astype(F32)
+        slots = range(i * 4 + (i == 3), i * 4 + 4)
+        wait_bytes(rs_buf.at[pl.ds(slots[0], len(slots))], rs_r.at[i])
+        for k in slots:
+            total = total + rs_buf[k].astype(F32)
     tb = total.astype(BF16)
 
     gs = (ga, gb)
@@ -284,11 +271,10 @@
     def ag1(half, d):
         blk = at_rows(half, x, y)
         dev = seq_at(0, d) if half else seq_at(d, 0)
-        n = half * 16 + d
-        return remote(blk, blk, ag_s.at[n], ag_r.at[n], (dev, c))
+        return remote(blk, blk, ag_s.at[half], ag_r.at[half * 6 + d - 1], (dev, c))
 
     def ag2(half, d, e):
-        n = half * 16 + 4 + d * 3 + e - 1
+        n = half * 6 + (3, 4, 5, 4)[d]
         if (d, e) == (2, 2):
             blk = at_rows(half, x, y)
             dev = seq_at(2, 2)
@@ -298,30 +284,42 @@
         else:
             blk = at_rows(1, x, (y + NY - d) % NY)
             dev = seq_at(e, 0)
-        return remote(blk, blk, ag_s.at[n], ag_r.at[n], (dev, c))
+        return remote(blk, blk, ag_s.at[half], ag_r.at[n], (dev, c))
 
     for d in ORDER:
         for half in range(2):
             ag1(half, d).start()
     for half in range(2):
         ag2(half, 2, 2).start()
+    for d in ORDER:
+        cnty_copy(d).start()
     for d in (2, 1, 3):
         for half in range(2):
             ag2(half, 0, d).start()
     for d in ORDER:
         for half in range(2):
-            ag1(half, d).wait()
+            ag1(half, d).wait_recv()
             for e in (2, 1, 3):
                 if (d, e) != (2, 2):
                     ag2(half, d, e).start()
 
+    wait_bytes(cnt_yb.at[pl.ds(1, 3)], cnt_r.at[1])
+    tot = cnt_y[...] + cnt_yb[1] + cnt_yb[2] + cnt_yb[3]
+    inv = 1.0 / jnp.maximum(tot, 1.0)
+    inv_ref[...] = inv
+    mult_ref[...] = inv * (1.0 / jnp.sqrt(F32(D)))
+    bias_ref[...] = (
+        jnp.where(tot > 0, jnp.log(1.0 + tot), F32(-1e9)).astype(BF16).astype(F32)
+    )
+
     top = den = att = None
-    for dists in ((0,), (1, 3), (2,)):
+    for step, dists in enumerate(((0,), (1, 3), (2,))):
         keys, rows = [], []
+        for half in range(2):
+            size = 3 * ROWS * len(dists)
+            wait_bytes(gs[half].at[pl.ds(0, size), :], ag_r.at[half * 6 + 3 + step])
         for d in dists:
             for half in range(2):
-                for e in ORDER:
-                    ag2(half, d, e).wait()
                 g = (y + NY - d) % NY if half else (x + NX - d) % NX
                 keys.append(gs[half][pl.ds(pl.multiple_of(g * MB, MB), MB), :])
                 rows += [half * 8 + g * 2, half * 8 + g * 2 + 1]
@@ -348,24 +346,31 @@
                 e = jnp.exp(sc[:, (2 * n + j) * 128 : (2 * n + j + 1) * 128] - top)
                 den = e if den is None else den + e
                 ps.append((e * inv_ref[pl.ds(r, 1), :]).astype(BF16))
-            pv = jnp.dot(jnp.concatenate(ps, axis=1), kb, preferred_element_type=F32)
+            p = jnp.concatenate(ps, axis=1)
+            pv = jnp.dot(p, kb, preferred_element_type=F32)
             att = pv if att is None else att + pv
     att = (att / jnp.sum(den, axis=1, keepdims=True)).astype(BF16)
 
-    hid = jnp.maximum(hc[...] + nt_dot(wt[:, D:], att), 0.0)
-    hid = hid * jnp.concatenate([wcol[...], wcol[...]], axis=1)
-    row = jnp.sum(hid, axis=0, keepdims=True)
+    row = 0.0
+    for k in range(2):
+        part = slice(k * (HID // 2), (k + 1) * (HID // 2))
+        hid = jnp.maximum(hc[part, :] + nt_dot(wt[part, D:], att), 0.0)
+        hid = hid * jnp.concatenate([wcol[part, :], wcol[part, :]], axis=1)
+        row = row + jnp.sum(hid, axis=0, keepdims=True)
     for j in range(NCAND):
         out_send[j, :, :32] = row[:, j * 32 : (j + 1) * 32]
-    back = []
     for j in range(1, NCAND):
         peer = (c + j) % NCAND
-        cp = remote(out_send.at[peer], out_buf.at[c], out_s.at[j], out_r.at[j], (s, peer))
-        cp.start()
-        back.append(cp)
+        remote(out_send.at[peer], out_buf.at[c], out_s.at[0], out_s.at[1], (s, peer)).start()
     out_buf[c] = out_send[c]
-    for cp in back:
-        cp.wait()
+    wait_bytes(mine.at[pl.ds(0, 7)], cand_s.at[0])
+    wait_bytes(cnt_xb.at[pl.ds(1, 3)], cnt_s.at[0])
+    wait_bytes(cnt_yb.at[pl.ds(1, 3)], cnt_s.at[1])
+    wait_bytes(rs_buf.at[pl.ds(0, 15)], rs_s.at[0])
+    for half in range(2):
+        wait_bytes(gs[half].at[pl.ds(0, 15 * ROWS), :], ag_s.at[half])
+    wait_bytes(out_buf.at[pl.ds(0, 7)], out_s.at[0])
+    wait_bytes(out_buf.at[pl.ds(0, 7)], out_s.at[1])
     out_ref[...] = out_buf[:, 0, :32]
 
 
@@ -393,7 +398,7 @@
             pltpu.VMEM((SLOTS, 2 * D), BF16),
             pltpu.VMEM((16, SLOTS), BF16),
             pltpu.VMEM((16, SLOTS), BF16),
-            pltpu.VMEM((MB, 2 * D), F32),
+            pltpu.VMEM((2, 2 * ROWS, 2 * D), F32),
             pltpu.VMEM((ROWS, 2 * D), F32),
             pltpu.VMEM((4, MB, 2 * D), BF16),
             pltpu.VMEM((16, ROWS, 2 * D), BF16),
@@ -417,16 +422,14 @@
             pltpu.VMEM((256, 1024), F32),
             dma((CHUNKS,)),
             dma((9,)),
-            dma((8,)),
-            dma((8,)),
-            dma((8,)),
-            dma((8,)),
-            dma((16,)),
-            dma((16,)),
-            dma((32,)),
-            dma((32,)),
-            dma((8,)),
-            dma((8,)),
+            dma((2,)),
+            dma((2,)),
+            dma((2,)),
+            dma((1,)),
+            dma((4,)),
+            dma((2,)),
+            dma((12,)),
+            dma((2,)),
         ],
         compiler_params=pltpu.CompilerParams(collective_id=0, has_side_effects=True),
         name="fused",

time: 36.1 us -> 32.4 us (0.90)
  Pallas kernels: 34.8 us -> 31 us
    pallas_call x1, Pallas kernels: 34.8 us -> 31 us  [on_device(): pl.pallas_call(kernel, out_shape=pltpu.VMEM((8, 32), F32), in_specs=[pl.B...]
where the time goes in v4:
time: 32.4 us; the launch traced here: 32.3 us
  Pallas kernels  31 us (96%)
  between operations  0.66 us (2%)
  local copies, waits for them, and re-layouts  0.6 us (2%)
    pallas_call x1, Pallas kernels, on_device(): pl.pallas_call(kernel, out_shape=pltpu.VMEM((8, 32), F32), in_specs=[pl.B...  31 us

profile of v4, /device:TPU:1, one launch (start us, length us, event | category | flops | bytes accessed | tf_op | source)
XLA Modules:
  0.0 32.3 jit_solution(5697528762935131273)
XLA Ops:
  0.7 31.0 %fused.1 = f32[8,32]{1,0:T(8,128)S(1)} custom-call(s32[1,1]{1,0:T(1,128)S(6)} %copy.12.len_hbm, f32[1,8192,128]{2,1,0:T(8,128)} %beh_hbm.1, s32[1,8192]{1,0:T(1,128)} %ids_hbm.1, s32[64,128]{1,0:T(8,128)} %bitcast.3, bf16[8,32,128]{2,1,0:T(8,128)(2,1)} %cand_hbm.1, bf16[128,128]{1,0:T(8,128)(2,1)} %wq_hbm.1, bf16[128,128]{1,0:T(8,128)(2,1)} %wk_hbm.1, ...), custom_call_target="tpu_custom_call" | custom-call | tf_op jit(solution)/shard_map/fused/pallas_call | solution.py:382
  31.7 0.6 %copy.11 = f32[8,32]{1,0:T(8,128)} copy(f32[8,32]{1,0:T(8,128)S(1)} %fused.1) | data formatting | bytes 2048

commit v5 on v4

--- a/solution.py
+++ b/solution.py
@@ -36,11 +36,13 @@
 
 
 SETS = (
-    ((2, 2), (1, 2), (3, 2), (2, 3)),
-    ((1, 3), (3, 3), (0, 2), (2, 1)),
-    ((0, 3), (1, 1), (3, 1), (2, 0)),
-    ((0, 0), (1, 0), (3, 0), (0, 1)),
+    ((2, 3), (1, 2), (3, 2), (2, 1)),
+    ((1, 1), (1, 3), (3, 1), (3, 3)),
+    ((2, 2), (2, 0), (0, 2), (1, 0)),
+    ((0, 0), (3, 0), (0, 1), (0, 3)),
 )
+EARLY = ((2, 3), (2, 1), (2, 2), (2, 0), (0, 2))
+LATE = ((0, 1), (0, 3))
 ORDER = (1, 3, 2)
 
 
@@ -72,7 +74,9 @@
     acc,
     own,
     s_send,
-    rs_buf,
+    add_buf,
+    add_send,
+    fin_buf,
     cnt_x,
     cnt_xb,
     cnt_y,
@@ -97,7 +101,8 @@
     cnt_s,
     cnt_r,
     rs_s,
-    rs_r,
+    add_r,
+    fin_r,
     ag_s,
     ag_r,
     out_s,
@@ -202,14 +207,52 @@
         s_send[0, n * 2 * ROWS : (n + 1) * 2 * ROWS, :] = acc[n].astype(BF16)
     cnt_x[...] = counts
 
-    def rs_copy(i, j):
-        return remote(
-            s_send.at[i, pl.ds(j * ROWS, ROWS), :],
-            rs_buf.at[i * 4 + j],
-            rs_s.at[0],
-            rs_r.at[i],
-            (seq_at(*SETS[i][j]), c),
-        )
+    def flip(half, p, q):
+        return (q, p) if half else (p, q)
+
+    def rs_start(i):
+        for j, offset in enumerate(SETS[i]):
+            for half in range(2):
+                p, q = flip(half, *offset)
+                src = s_send.at[i, pl.ds(j * ROWS, ROWS), pl.ds(half * D, D)]
+                if p % 2 and q:
+                    remote(
+                        src,
+                        add_buf.at[half, p // 2 * 3 + q - 1],
+                        rs_s.at[0],
+                        add_r.at[half],
+                        (seq_at(*flip(half, 0, q)), c),
+                    ).start()
+                elif (p, q) in EARLY:
+                    dst = fin_buf.at[half, EARLY.index((p, q))]
+                    remote(
+                        src, dst, rs_s.at[1], fin_r.at[half], (seq_at(*offset), c)
+                    ).start()
+                elif (p, q) in LATE:
+                    dst = fin_buf.at[half, 5 + LATE.index((p, q))]
+                    remote(
+                        src, dst, rs_s.at[1], fin_r.at[2 + half], (seq_at(*offset), c)
+                    ).start()
+
+    def add_and_send():
+        for half in range(2):
+            wait_bytes(add_buf.at[half], add_r.at[half])
+            for n, p in enumerate((1, 3)):
+                offset = flip(half, p, 0)
+                i, j = next((i, z.index(offset)) for i, z in enumerate(SETS) if offset in z)
+                val = s_send[i, j * ROWS : (j + 1) * ROWS, half * D : (half + 1) * D].astype(F32)
+                for q in range(3):
+                    val = val + add_buf[half, n * 3 + q].astype(F32)
+                add_send[half, n] = val.astype(BF16)
+        for half in range(2):
+            for n, p in enumerate((1, 3)):
+                remote(
+                    add_send.at[half, n],
+                    fin_buf.at[half, 7 + n],
+                    rs_s.at[1],
+                    fin_r.at[2 + half],
+                    (seq_at(*flip(half, p, 0)), c),
+                ).start()
 
     def cntx_copy(d):
         return remote(cnt_x, cnt_xb.at[d], cnt_s.at[0], cnt_r.at[0], (seq_at(d, 0), c))
@@ -221,8 +264,7 @@
     pl.semaphore_wait(barrier, 22)
     for d in ORDER:
         cntx_copy(d).start()
-    for j in range(4):
-        rs_copy(0, j).start()
+    rs_start(0)
     for j in range(1, NCAND):
         peer = (c + j) % NCAND
         remote(cand_ref.at[peer], mine.at[c], cand_s.at[0], cand_s.at[1], (s, peer)).start()
@@ -234,9 +276,8 @@
             s_send[i, n * 2 * ROWS : (n + 1) * 2 * ROWS, :] = val[n].astype(BF16)
         if i == 3:
             own[...] = val[0][:ROWS]
-        for j in range(4):
-            if SETS[i][j] != (0, 0):
-                rs_copy(i, j).start()
+        rs_start(i)
+    add_and_send()
 
     for cp in ops[4:]:
         cp.wait()
@@ -251,13 +292,17 @@
     wait_bytes(cnt_xb.at[pl.ds(1, 3)], cnt_r.at[0])
     cnt_y[...] = cnt_x[...] + cnt_xb[1] + cnt_xb[2] + cnt_xb[3]
 
-    total = own[...]
-    for i in range(4):
-        slots = range(i * 4 + (i == 3), i * 4 + 4)
-        wait_bytes(rs_buf.at[pl.ds(slots[0], len(slots))], rs_r.at[i])
-        for k in slots:
-            total = total + rs_buf[k].astype(F32)
-    tb = total.astype(BF16)
+    halves = []
+    for half in range(2):
+        total = own[:, half * D : (half + 1) * D]
+        wait_bytes(fin_buf.at[half, pl.ds(0, 5)], fin_r.at[half])
+        for k in range(5):
+            total = total + fin_buf[half, k].astype(F32)
+        halves.append(total)
+    for half in range(2):
+        wait_bytes(fin_buf.at[half, pl.ds(5, 4)], fin_r.at[2 + half])
+        for k in range(5, 9):
+            halves[half] = halves[half] + fin_buf[half, k].astype(F32)
 
     gs = (ga, gb)
 
@@ -265,44 +310,28 @@
         p = py * NX + px if half else px * NY + py
         return gs[half].at[pl.ds(pl.multiple_of(p * ROWS, ROWS), ROWS), :]
 
-    at_rows(0, x, y)[...] = tb[:, :128]
-    at_rows(1, x, y)[...] = tb[:, 128:]
-
-    def ag1(half, d):
-        blk = at_rows(half, x, y)
-        dev = seq_at(0, d) if half else seq_at(d, 0)
-        return remote(blk, blk, ag_s.at[half], ag_r.at[half * 6 + d - 1], (dev, c))
-
-    def ag2(half, d, e):
-        n = half * 6 + (3, 4, 5, 4)[d]
-        if (d, e) == (2, 2):
-            blk = at_rows(half, x, y)
-            dev = seq_at(2, 2)
-        elif half == 0:
-            blk = at_rows(0, (x + NX - d) % NX, y)
-            dev = seq_at(0, e)
-        else:
-            blk = at_rows(1, x, (y + NY - d) % NY)
-            dev = seq_at(e, 0)
+    for half in range(2):
+        at_rows(half, x, y)[...] = halves[half].astype(BF16)
+
+    def ag_copy(half, via, p, q):
+        blk = at_rows(half, *[(z + 4 - w) % 4 for z, w in zip((x, y), flip(half, via, 0))])
+        n = half * 5 + (0 if p == 0 else 1 if p == 2 else 2 if q else 3 + p // 2)
+        dev = seq_at(*flip(half, p - via, q))
         return remote(blk, blk, ag_s.at[half], ag_r.at[n], (dev, c))
 
-    for d in ORDER:
+    for p in ORDER:
         for half in range(2):
-            ag1(half, d).start()
-    for half in range(2):
-        ag2(half, 2, 2).start()
+            ag_copy(half, 0, p, 0).start()
+    for p, q in ((2, 2), (1, 2), (3, 2), (2, 1), (2, 3), (0, 2), (0, 1), (0, 3)):
+        for half in range(2):
+            ag_copy(half, 0, p, q).start()
     for d in ORDER:
         cnty_copy(d).start()
-    for d in (2, 1, 3):
+    for p in (1, 3):
         for half in range(2):
-            ag2(half, 0, d).start()
-    for d in ORDER:
-        for half in range(2):
-            ag1(half, d).wait_recv()
-            for e in (2, 1, 3):
-                if (d, e) != (2, 2):
-                    ag2(half, d, e).start()
-
+            ag_copy(half, 0, p, 0).wait_recv()
+            for q in (1, 3):
+                ag_copy(half, p, p, q).start()
     wait_bytes(cnt_yb.at[pl.ds(1, 3)], cnt_r.at[1])
     tot = cnt_y[...] + cnt_yb[1] + cnt_yb[2] + cnt_yb[3]
     inv = 1.0 / jnp.maximum(tot, 1.0)
@@ -313,11 +342,11 @@
     )
 
     top = den = att = None
-    for step, dists in enumerate(((0,), (1, 3), (2,))):
+    for step, dists in enumerate(((0,), (2,), (1, 3))):
         keys, rows = [], []
         for half in range(2):
-            size = 3 * ROWS * len(dists)
-            wait_bytes(gs[half].at[pl.ds(0, size), :], ag_r.at[half * 6 + 3 + step])
+            size = (3, 4, 6)[step] * ROWS
+            wait_bytes(gs[half].at[pl.ds(0, size), :], ag_r.at[half * 5 + step])
         for d in dists:
             for half in range(2):
                 g = (y + NY - d) % NY if half else (x + NX - d) % NX
@@ -366,7 +395,8 @@
     wait_bytes(mine.at[pl.ds(0, 7)], cand_s.at[0])
     wait_bytes(cnt_xb.at[pl.ds(1, 3)], cnt_s.at[0])
     wait_bytes(cnt_yb.at[pl.ds(1, 3)], cnt_s.at[1])
-    wait_bytes(rs_buf.at[pl.ds(0, 15)], rs_s.at[0])
+    wait_bytes(add_buf, rs_s.at[0])
+    wait_bytes(fin_buf, rs_s.at[1])
     for half in range(2):
         wait_bytes(gs[half].at[pl.ds(0, 15 * ROWS), :], ag_s.at[half])
     wait_bytes(out_buf.at[pl.ds(0, 7)], out_s.at[0])
@@ -401,7 +431,9 @@
             pltpu.VMEM((2, 2 * ROWS, 2 * D), F32),
             pltpu.VMEM((ROWS, 2 * D), F32),
             pltpu.VMEM((4, MB, 2 * D), BF16),
-            pltpu.VMEM((16, ROWS, 2 * D), BF16),
+            pltpu.VMEM((2, 6, ROWS, D), BF16),
+            pltpu.VMEM((2, 2, ROWS, D), BF16),
+            pltpu.VMEM((2, 9, ROWS, D), BF16),
             pltpu.VMEM((16, 128), F32),
             pltpu.VMEM((4, 16, 128), F32),
             pltpu.VMEM((16, 128), F32),
@@ -425,10 +457,11 @@
             dma((2,)),
             dma((2,)),
             dma((2,)),
-            dma((1,)),
+            dma((2,)),
+            dma((2,)),
             dma((4,)),
             dma((2,)),
-            dma((12,)),
+            dma((10,)),
             dma((2,)),
         ],
         compiler_params=pltpu.CompilerParams(collective_id=0, has_side_effects=True),

time: 32.4 us -> 32.5 us (level)
  no operation moved by 1% of the time
where the time goes in v5:
time: 32.5 us; the launch traced here: 32.4 us
  Pallas kernels  31.1 us (96%)
  between operations  0.66 us (2%)
  local copies, waits for them, and re-layouts  0.6 us (2%)
    pallas_call x1, Pallas kernels, on_device(): pl.pallas_call(kernel, out_shape=pltpu.VMEM((8, 32), F32), in_specs=[pl.B...  31.1 us

profile of v5, /device:TPU:1, one launch (start us, length us, event | category | flops | bytes accessed | tf_op | source)
XLA Modules:
  0.0 32.4 jit_solution(5838853755641001926)
XLA Ops:
  0.7 31.1 %fused.1 = f32[8,32]{1,0:T(8,128)S(1)} custom-call(s32[1,1]{1,0:T(1,128)S(6)} %copy.12.len_hbm, f32[1,8192,128]{2,1,0:T(8,128)} %beh_hbm.1, s32[1,8192]{1,0:T(1,128)} %ids_hbm.1, s32[64,128]{1,0:T(8,128)} %bitcast.3, bf16[8,32,128]{2,1,0:T(8,128)(2,1)} %cand_hbm.1, bf16[128,128]{1,0:T(8,128)(2,1)} %wq_hbm.1, bf16[128,128]{1,0:T(8,128)(2,1)} %wk_hbm.1, ...), custom_call_target="tpu_custom_call" | custom-call | tf_op jit(solution)/shard_map/fused/pallas_call | solution.py:412
  31.8 0.6 %copy.11 = f32[8,32]{1,0:T(8,128)} copy(f32[8,32]{1,0:T(8,128)S(1)} %fused.1) | data formatting | bytes 2048

commit v6 on v5

--- a/solution.py
+++ b/solution.py
@@ -36,13 +36,11 @@
 
 
 SETS = (
-    ((2, 3), (1, 2), (3, 2), (2, 1)),
-    ((1, 1), (1, 3), (3, 1), (3, 3)),
-    ((2, 2), (2, 0), (0, 2), (1, 0)),
+    ((2, 2), (2, 1), (2, 3), (1, 2)),
+    ((3, 2), (1, 1), (1, 3), (3, 1)),
+    ((3, 3), (2, 0), (0, 2), (1, 0)),
     ((0, 0), (3, 0), (0, 1), (0, 3)),
 )
-EARLY = ((2, 3), (2, 1), (2, 2), (2, 0), (0, 2))
-LATE = ((0, 1), (0, 3))
 ORDER = (1, 3, 2)
 
 
@@ -176,10 +174,17 @@
         return jnp.concatenate(parts, axis=0)
 
     def block_sums(i, k0, kc):
+        rows = jnp.concatenate([rhs[0, k0 : k0 + kc, :], rhs[1, k0 : k0 + kc, :]], axis=1)
         return [
-            jnp.dot(onehot(owners, k0, kc), rhs[k0 : k0 + kc, :], preferred_element_type=F32)
+            jnp.dot(onehot(owners, k0, kc), rows, preferred_element_type=F32)
             for owners in (SETS[i][:2], SETS[i][2:])
         ]
+
+    def put_sums(i, n, val):
+        for half in range(2):
+            s_send[half, i, n * 2 * ROWS : (n + 1) * 2 * ROWS, :] = val[
+                :, half * D : (half + 1) * D
+            ].astype(BF16)
 
     lane = lax.broadcasted_iota(jnp.int32, (128, 128), 1).astype(F32).astype(BF16)
     a_iota = lax.broadcasted_iota(jnp.int32, (16, CH), 0).astype(F32).astype(BF16)
@@ -191,8 +196,8 @@
         for g in range(k * (CH // 128), (k + 1) * (CH // 128)):
             upper = jnp.broadcast_to(half_t[:, g : g + 1], (128, 128)) != zero
             v = beh_v[g * 128 : (g + 1) * 128, :].astype(BF16)
-            rhs[g * 128 : (g + 1) * 128, :128] = jnp.where(upper, zero, v)
-            rhs[g * 128 : (g + 1) * 128, 128:] = jnp.where(upper, v, zero)
+            rhs[0, g * 128 : (g + 1) * 128, :] = jnp.where(upper, zero, v)
+            rhs[1, g * 128 : (g + 1) * 128, :] = jnp.where(upper, v, zero)
             low = jnp.broadcast_to(low_t[:, g : g + 1], (128, 128))
             bh.append(jnp.where(low == lane, BF16(1), zero))
         ab = jnp.broadcast_to(ahot_row[:, k * CH : (k + 1) * CH], (16, CH)).astype(BF16)
@@ -204,7 +209,7 @@
             else:
                 acc[n] += part
     for n in range(2):
-        s_send[0, n * 2 * ROWS : (n + 1) * 2 * ROWS, :] = acc[n].astype(BF16)
+        put_sums(0, n, acc[n])
     cnt_x[...] = counts
 
     def flip(half, p, q):
@@ -214,43 +219,37 @@
         for j, offset in enumerate(SETS[i]):
             for half in range(2):
                 p, q = flip(half, *offset)
-                src = s_send.at[i, pl.ds(j * ROWS, ROWS), pl.ds(half * D, D)]
-                if p % 2 and q:
+                src = s_send.at[half, i, pl.ds(j * ROWS, ROWS), :]
+                if p and q:
                     remote(
                         src,
-                        add_buf.at[half, p // 2 * 3 + q - 1],
+                        add_buf.at[half, p - 1, q - 1],
                         rs_s.at[0],
-                        add_r.at[half],
+                        add_r.at[half * 3 + p - 1],
                         (seq_at(*flip(half, 0, q)), c),
                     ).start()
-                elif (p, q) in EARLY:
-                    dst = fin_buf.at[half, EARLY.index((p, q))]
+                elif q:
+                    dst = fin_buf.at[half, q - 1]
                     remote(
                         src, dst, rs_s.at[1], fin_r.at[half], (seq_at(*offset), c)
                     ).start()
-                elif (p, q) in LATE:
-                    dst = fin_buf.at[half, 5 + LATE.index((p, q))]
-                    remote(
-                        src, dst, rs_s.at[1], fin_r.at[2 + half], (seq_at(*offset), c)
-                    ).start()
 
     def add_and_send():
-        for half in range(2):
-            wait_bytes(add_buf.at[half], add_r.at[half])
-            for n, p in enumerate((1, 3)):
+        for p in (2, 1, 3):
+            for half in range(2):
+                wait_bytes(add_buf.at[half, p - 1], add_r.at[half * 3 + p - 1])
                 offset = flip(half, p, 0)
                 i, j = next((i, z.index(offset)) for i, z in enumerate(SETS) if offset in z)
-                val = s_send[i, j * ROWS : (j + 1) * ROWS, half * D : (half + 1) * D].astype(F32)
+                val = s_send[half, i, j * ROWS : (j + 1) * ROWS, :].astype(F32)
                 for q in range(3):
-                    val = val + add_buf[half, n * 3 + q].astype(F32)
-                add_send[half, n] = val.astype(BF16)
-        for half in range(2):
-            for n, p in enumerate((1, 3)):
+                    val = val + add_buf[half, p - 1, q].astype(F32)
+                add_send[half, p - 1] = val.astype(BF16)
+            for half in range(2):
                 remote(
-                    add_send.at[half, n],
-                    fin_buf.at[half, 7 + n],
+                    add_send.at[half, p - 1],
+                    fin_buf.at[half, 2 + p],
                     rs_s.at[1],
-                    fin_r.at[2 + half],
+                    fin_r.at[half],
                     (seq_at(*flip(half, p, 0)), c),
                 ).start()
 
@@ -273,7 +272,7 @@
     for i in range(1, 4):
         val = block_sums(i, 0, SLOTS)
         for n in range(2):
-            s_send[i, n * 2 * ROWS : (n + 1) * 2 * ROWS, :] = val[n].astype(BF16)
+            put_sums(i, n, val[n])
         if i == 3:
             own[...] = val[0][:ROWS]
         rs_start(i)
@@ -295,14 +294,10 @@
     halves = []
     for half in range(2):
         total = own[:, half * D : (half + 1) * D]
-        wait_bytes(fin_buf.at[half, pl.ds(0, 5)], fin_r.at[half])
-        for k in range(5):
+        wait_bytes(fin_buf.at[half], fin_r.at[half])
+        for k in range(6):
             total = total + fin_buf[half, k].astype(F32)
         halves.append(total)
-    for half in range(2):
-        wait_bytes(fin_buf.at[half, pl.ds(5, 4)], fin_r.at[2 + half])
-        for k in range(5, 9):
-            halves[half] = halves[half] + fin_buf[half, k].astype(F32)
 
     gs = (ga, gb)
 
@@ -315,16 +310,29 @@
 
     def ag_copy(half, via, p, q):
         blk = at_rows(half, *[(z + 4 - w) % 4 for z, w in zip((x, y), flip(half, via, 0))])
-        n = half * 5 + (0 if p == 0 else 1 if p == 2 else 2 if q else 3 + p // 2)
+        n = half * 6 + ((0, 1, 2, 1)[p] if p == 0 or q else 2 + p)
         dev = seq_at(*flip(half, p - via, q))
         return remote(blk, blk, ag_s.at[half], ag_r.at[n], (dev, c))
 
     for p in ORDER:
         for half in range(2):
             ag_copy(half, 0, p, 0).start()
-    for p, q in ((2, 2), (1, 2), (3, 2), (2, 1), (2, 3), (0, 2), (0, 1), (0, 3)):
+    first = c % 2 == 0
+
+    def far(relayed):
+        for p, q in ((1, 2), (3, 2), (2, 1), (2, 3)):
+            for half in range(2):
+                if not relayed:
+                    ag_copy(half, 0, p, q).start()
+                elif relayed == p:
+                    ag_copy(half, p, p, q).start()
+
+    for half in range(2):
+        ag_copy(half, 0, 2, 2).start()
+    pl.when(first)(lambda: far(0))
+    for q in (2, 1, 3):
         for half in range(2):
-            ag_copy(half, 0, p, q).start()
+            ag_copy(half, 0, 0, q).start()
     for d in ORDER:
         cnty_copy(d).start()
     for p in (1, 3):
@@ -332,6 +340,10 @@
             ag_copy(half, 0, p, 0).wait_recv()
             for q in (1, 3):
                 ag_copy(half, p, p, q).start()
+        pl.when(jnp.logical_not(first))(lambda p=p: far(p))
+    for half in range(2):
+        ag_copy(half, 0, 2, 0).wait_recv()
+    pl.when(jnp.logical_not(first))(lambda: far(2))
     wait_bytes(cnt_yb.at[pl.ds(1, 3)], cnt_r.at[1])
     tot = cnt_y[...] + cnt_yb[1] + cnt_yb[2] + cnt_yb[3]
     inv = 1.0 / jnp.maximum(tot, 1.0)
@@ -342,11 +354,11 @@
     )
 
     top = den = att = None
-    for step, dists in enumerate(((0,), (2,), (1, 3))):
+    for step, dists in ((0, (0,)), (2, (2,)), (1, (1, 3))):
         keys, rows = [], []
         for half in range(2):
-            size = (3, 4, 6)[step] * ROWS
-            wait_bytes(gs[half].at[pl.ds(0, size), :], ag_r.at[half * 5 + step])
+            size = (3, 6, 3)[step] * ROWS
+            wait_bytes(gs[half].at[pl.ds(0, size), :], ag_r.at[half * 6 + step])
         for d in dists:
             for half in range(2):
                 g = (y + NY - d) % NY if half else (x + NX - d) % NX
@@ -425,15 +437,15 @@
             pltpu.VMEM((2 * D, HID), BF16),
             pltpu.VMEM((1, HID), F32),
             pltpu.VMEM((1, HID), F32),
-            pltpu.VMEM((SLOTS, 2 * D), BF16),
+            pltpu.VMEM((2, SLOTS, D), BF16),
             pltpu.VMEM((16, SLOTS), BF16),
             pltpu.VMEM((16, SLOTS), BF16),
             pltpu.VMEM((2, 2 * ROWS, 2 * D), F32),
             pltpu.VMEM((ROWS, 2 * D), F32),
-            pltpu.VMEM((4, MB, 2 * D), BF16),
+            pltpu.VMEM((2, 4, MB, D), BF16),
+            pltpu.VMEM((2, 3, 3, ROWS, D), BF16),
+            pltpu.VMEM((2, 3, ROWS, D), BF16),
             pltpu.VMEM((2, 6, ROWS, D), BF16),
-            pltpu.VMEM((2, 2, ROWS, D), BF16),
-            pltpu.VMEM((2, 9, ROWS, D), BF16),
             pltpu.VMEM((16, 128), F32),
             pltpu.VMEM((4, 16, 128), F32),
             pltpu.VMEM((16, 128), F32),
@@ -458,10 +470,10 @@
             dma((2,)),
             dma((2,)),
             dma((2,)),
-            dma((2,)),
-            dma((4,)),
-            dma((2,)),
-            dma((10,)),
+            dma((6,)),
+            dma((2,)),
+            dma((2,)),
+            dma((12,)),
             dma((2,)),
         ],
         compiler_params=pltpu.CompilerParams(collective_id=0, has_side_effects=True),

time: 32.5 us -> 31.8 us (0.978)
  Pallas kernels: 31.1 us -> 30.4 us
    pallas_call x1, Pallas kernels: 31.1 us -> 30.4 us  [on_device(): pl.pallas_call(kernel, out_shape=pltpu.VMEM((8, 32), F32), in_specs=[pl.B...]
where the time goes in v6:
time: 31.8 us; the launch traced here: 31.7 us
  Pallas kernels  30.4 us (96%)
  between operations  0.66 us (2%)
  local copies, waits for them, and re-layouts  0.6 us (2%)
    pallas_call x1, Pallas kernels, on_device(): pl.pallas_call(kernel, out_shape=pltpu.VMEM((8, 32), F32), in_specs=[pl.B...  30.4 us

profile of v6, /device:TPU:1, one launch (start us, length us, event | category | flops | bytes accessed | tf_op | source)
XLA Modules:
  0.0 31.7 jit_solution(4872225781811574959)
XLA Ops:
  0.7 30.4 %fused.1 = f32[8,32]{1,0:T(8,128)S(1)} custom-call(s32[1,1]{1,0:T(1,128)S(6)} %copy.12.len_hbm, f32[1,8192,128]{2,1,0:T(8,128)} %beh_hbm.1, s32[1,8192]{1,0:T(1,128)} %ids_hbm.1, s32[64,128]{1,0:T(8,128)} %bitcast.3, bf16[8,32,128]{2,1,0:T(8,128)(2,1)} %cand_hbm.1, bf16[128,128]{1,0:T(8,128)(2,1)} %wq_hbm.1, bf16[128,128]{1,0:T(8,128)(2,1)} %wk_hbm.1, ...), custom_call_target="tpu_custom_call" | custom-call | tf_op jit(solution)/shard_map/fused/pallas_call | solution.py:424
  31.1 0.6 %copy.11 = f32[8,32]{1,0:T(8,128)} copy(f32[8,32]{1,0:T(8,128)S(1)} %fused.1) | data formatting | bytes 2048

commit v7 on v6

--- a/solution.py
+++ b/solution.py
@@ -42,6 +42,7 @@
     ((0, 0), (3, 0), (0, 1), (0, 3)),
 )
 ORDER = (1, 3, 2)
+LOG2E = 1.4426950408889634
 
 
 def kernel(
@@ -90,7 +91,6 @@
     out_send,
     out_buf,
     inv_ref,
-    mult_ref,
     bias_ref,
     sc,
     load_sem,
@@ -283,7 +283,7 @@
     wait_bytes(mine.at[pl.ds(0, 7)], cand_s.at[1])
     cands = mine[...].reshape(256, 128)
     q = jnp.dot(cands, wq_ref[...], preferred_element_type=F32).astype(BF16)
-    q2[...] = nt_dot(q, wk_ref[...]).astype(BF16)
+    q2[...] = (nt_dot(q, wk_ref[...]) * (LOG2E / D**0.5)).astype(BF16)
     wt[...] = wh_ref[...].astype(F32).T.astype(BF16)
     bcol[...] = jnp.broadcast_to(bh_ref[...], (128, HID)).T
     wcol[...] = jnp.broadcast_to(wo_ref[...], (128, HID)).T
@@ -320,7 +320,7 @@
     first = c % 2 == 0
 
     def far(relayed):
-        for p, q in ((1, 2), (3, 2), (2, 1), (2, 3)):
+        for p, q in ((1, 2), (3, 2), (2, 1), (2, 3), (1, 1), (1, 3), (3, 1), (3, 3)):
             for half in range(2):
                 if not relayed:
                     ag_copy(half, 0, p, q).start()
@@ -338,8 +338,6 @@
     for p in (1, 3):
         for half in range(2):
             ag_copy(half, 0, p, 0).wait_recv()
-            for q in (1, 3):
-                ag_copy(half, p, p, q).start()
         pl.when(jnp.logical_not(first))(lambda p=p: far(p))
     for half in range(2):
         ag_copy(half, 0, 2, 0).wait_recv()
@@ -347,50 +345,42 @@
     wait_bytes(cnt_yb.at[pl.ds(1, 3)], cnt_r.at[1])
     tot = cnt_y[...] + cnt_yb[1] + cnt_yb[2] + cnt_yb[3]
     inv = 1.0 / jnp.maximum(tot, 1.0)
+    bias = jnp.where(tot > 0, jnp.log(1.0 + tot), F32(-1e9)).astype(BF16).astype(F32)
     inv_ref[...] = inv
-    mult_ref[...] = inv * (1.0 / jnp.sqrt(F32(D)))
-    bias_ref[...] = (
-        jnp.where(tot > 0, jnp.log(1.0 + tot), F32(-1e9)).astype(BF16).astype(F32)
-    )
-
-    top = den = att = None
-    for step, dists in ((0, (0,)), (2, (2,)), (1, (1, 3))):
-        keys, rows = [], []
+    bias_ref[...] = bias * LOG2E
+
+    for step in range(3):
         for half in range(2):
             size = (3, 6, 3)[step] * ROWS
             wait_bytes(gs[half].at[pl.ds(0, size), :], ag_r.at[half * 6 + step])
-        for d in dists:
-            for half in range(2):
-                g = (y + NY - d) % NY if half else (x + NX - d) % NX
-                keys.append(gs[half][pl.ds(pl.multiple_of(g * MB, MB), MB), :])
-                rows += [half * 8 + g * 2, half * 8 + g * 2 + 1]
-        new = None
-        for n, kb in enumerate(keys):
-            raw = nt_dot(q2[...], kb)
-            for j in range(2):
-                r = rows[2 * n + j]
-                t = raw[:, j * 128 : (j + 1) * 128] * mult_ref[pl.ds(r, 1), :]
-                t = t + bias_ref[pl.ds(r, 1), :]
-                sc[:, (2 * n + j) * 128 : (2 * n + j + 1) * 128] = t
-                new = t if new is None else jnp.maximum(new, t)
-        new = jnp.broadcast_to(jnp.max(new, axis=1, keepdims=True), (256, 128))
-        if top is not None:
-            new = jnp.maximum(top, new)
-            alpha = jnp.exp(top - new)
-            den = den * alpha
-            att = att * alpha
-        top = new
-        for n, kb in enumerate(keys):
-            ps = []
-            for j in range(2):
-                r = rows[2 * n + j]
-                e = jnp.exp(sc[:, (2 * n + j) * 128 : (2 * n + j + 1) * 128] - top)
-                den = e if den is None else den + e
-                ps.append((e * inv_ref[pl.ds(r, 1), :]).astype(BF16))
-            p = jnp.concatenate(ps, axis=1)
-            pv = jnp.dot(p, kb, preferred_element_type=F32)
-            att = pv if att is None else att + pv
-    att = (att / jnp.sum(den, axis=1, keepdims=True)).astype(BF16)
+    atts = []
+    for m in range(2):
+        part = slice(m * 128, (m + 1) * 128)
+        top = None
+        for half in range(2):
+            for n in range(4):
+                raw = nt_dot(q2[part, :], gs[half][n * MB : (n + 1) * MB, :])
+                for j in range(2):
+                    r = half * 8 + n * 2 + j
+                    t = raw[:, j * 128 : (j + 1) * 128] * inv_ref[r : r + 1, :]
+                    t = t + bias_ref[r : r + 1, :]
+                    sc[part, r * 128 : (r + 1) * 128] = t
+                    top = t if top is None else jnp.maximum(top, t)
+        top = jnp.broadcast_to(jnp.max(top, axis=1, keepdims=True), (128, 128))
+        att = den = None
+        for half in range(2):
+            for n in range(4):
+                ps = []
+                for j in range(2):
+                    r = half * 8 + n * 2 + j
+                    e = jnp.exp2(sc[part, r * 128 : (r + 1) * 128] - top)
+                    den = e if den is None else den + e
+                    ps.append((e * inv_ref[r : r + 1, :]).astype(BF16))
+                kb = gs[half][n * MB : (n + 1) * MB, :]
+                pv = jnp.dot(jnp.concatenate(ps, axis=1), kb, preferred_element_type=F32)
+                att = pv if att is None else att + pv
+        atts.append((att / jnp.sum(den, axis=1, keepdims=True)).astype(BF16))
+    att = jnp.concatenate(atts, axis=0)
 
     row = 0.0
     for k in range(2):
@@ -462,8 +452,7 @@
             pltpu.VMEM((8, 1, 128), F32),
             pltpu.VMEM((16, 128), F32),
             pltpu.VMEM((16, 128), F32),
-            pltpu.VMEM((16, 128), F32),
-            pltpu.VMEM((256, 1024), F32),
+            pltpu.VMEM((256, 2048), F32),
             dma((CHUNKS,)),
             dma((9,)),
             dma((2,)),

time: 31.8 us -> 32.2 us (1.013)
  Pallas kernels: 30.4 us -> 30.8 us
    pallas_call x1, Pallas kernels: 30.4 us -> 30.8 us  [on_device(): pl.pallas_call(kernel, out_shape=pltpu.VMEM((8, 32), F32), in_specs=[pl.B...]
where the time goes in v7:
time: 32.2 us; the launch traced here: 32.1 us
  Pallas kernels  30.8 us (96%)
  between operations  0.66 us (2%)
  local copies, waits for them, and re-layouts  0.6 us (2%)
    pallas_call x1, Pallas kernels, on_device(): pl.pallas_call(kernel, out_shape=pltpu.VMEM((8, 32), F32), in_specs=[pl.B...  30.8 us

profile of v7, /device:TPU:1, one launch (start us, length us, event | category | flops | bytes accessed | tf_op | source)
XLA Modules:
  0.0 32.1 jit_solution(12079025260086526315)
XLA Ops:
  0.7 30.8 %fused.1 = f32[8,32]{1,0:T(8,128)S(1)} custom-call(s32[1,1]{1,0:T(1,128)S(6)} %copy.12.len_hbm, f32[1,8192,128]{2,1,0:T(8,128)} %beh_hbm.1, s32[1,8192]{1,0:T(1,128)} %ids_hbm.1, s32[64,128]{1,0:T(8,128)} %bitcast.3, bf16[8,32,128]{2,1,0:T(8,128)(2,1)} %cand_hbm.1, bf16[128,128]{1,0:T(8,128)(2,1)} %wq_hbm.1, bf16[128,128]{1,0:T(8,128)(2,1)} %wk_hbm.1, ...), custom_call_target="tpu_custom_call" | custom-call | tf_op jit(solution)/shard_map/fused/pallas_call | solution.py:414
  31.5 0.6 %copy.11 = f32[8,32]{1,0:T(8,128)} copy(f32[8,32]{1,0:T(8,128)S(1)} %fused.1) | data formatting | bytes 2048

commit v8 on v6

--- a/solution.py
+++ b/solution.py
@@ -261,8 +261,6 @@
 
     ops[3].wait()
     pl.semaphore_wait(barrier, 22)
-    for d in ORDER:
-        cntx_copy(d).start()
     rs_start(0)
     for j in range(1, NCAND):
         peer = (c + j) % NCAND
@@ -276,6 +274,9 @@
         if i == 3:
             own[...] = val[0][:ROWS]
         rs_start(i)
+        if i == 1:
+            for d in ORDER:
+                cntx_copy(d).start()
     add_and_send()
 
     for cp in ops[4:]:

time: 31.8 us -> 31.9 us (level)
  no operation moved by 1% of the time
where the time goes in v8:
time: 31.9 us; the launch traced here: 31.8 us
  Pallas kernels  30.6 us (96%)
  between operations  0.66 us (2%)
  local copies, waits for them, and re-layouts  0.6 us (2%)
    pallas_call x1, Pallas kernels, on_device(): pl.pallas_call(kernel, out_shape=pltpu.VMEM((8, 32), F32), in_specs=[pl.B...  30.6 us

profile of v8, /device:TPU:1, one launch (start us, length us, event | category | flops | bytes accessed | tf_op | source)
XLA Modules:
  0.0 31.8 jit_solution(12001070482042212145)
XLA Ops:
  0.7 30.6 %fused.1 = f32[8,32]{1,0:T(8,128)S(1)} custom-call(s32[1,1]{1,0:T(1,128)S(6)} %copy.12.len_hbm, f32[1,8192,128]{2,1,0:T(8,128)} %beh_hbm.1, s32[1,8192]{1,0:T(1,128)} %ids_hbm.1, s32[64,128]{1,0:T(8,128)} %bitcast.3, bf16[8,32,128]{2,1,0:T(8,128)(2,1)} %cand_hbm.1, bf16[128,128]{1,0:T(8,128)(2,1)} %wq_hbm.1, bf16[128,128]{1,0:T(8,128)(2,1)} %wk_hbm.1, ...), custom_call_target="tpu_custom_call" | custom-call | tf_op jit(solution)/shard_map/fused/pallas_call | solution.py:425
  31.2 0.6 %copy.11 = f32[8,32]{1,0:T(8,128)} copy(f32[8,32]{1,0:T(8,128)S(1)} %fused.1) | data formatting | bytes 2048

commit v9 on v6

--- a/solution.py
+++ b/solution.py
@@ -42,6 +42,7 @@
     ((0, 0), (3, 0), (0, 1), (0, 3)),
 )
 ORDER = (1, 3, 2)
+LOG2E = 1.4426950408889634
 
 
 def kernel(
@@ -90,7 +91,6 @@
     out_send,
     out_buf,
     inv_ref,
-    mult_ref,
     bias_ref,
     sc,
     load_sem,
@@ -283,7 +283,7 @@
     wait_bytes(mine.at[pl.ds(0, 7)], cand_s.at[1])
     cands = mine[...].reshape(256, 128)
     q = jnp.dot(cands, wq_ref[...], preferred_element_type=F32).astype(BF16)
-    q2[...] = nt_dot(q, wk_ref[...]).astype(BF16)
+    q2[...] = (nt_dot(q, wk_ref[...]) * (LOG2E / D**0.5)).astype(BF16)
     wt[...] = wh_ref[...].astype(F32).T.astype(BF16)
     bcol[...] = jnp.broadcast_to(bh_ref[...], (128, HID)).T
     wcol[...] = jnp.broadcast_to(wo_ref[...], (128, HID)).T
@@ -348,10 +348,8 @@
     tot = cnt_y[...] + cnt_yb[1] + cnt_yb[2] + cnt_yb[3]
     inv = 1.0 / jnp.maximum(tot, 1.0)
     inv_ref[...] = inv
-    mult_ref[...] = inv * (1.0 / jnp.sqrt(F32(D)))
-    bias_ref[...] = (
-        jnp.where(tot > 0, jnp.log(1.0 + tot), F32(-1e9)).astype(BF16).astype(F32)
-    )
+    bias = jnp.where(tot > 0, jnp.log(1.0 + tot), F32(-1e9)).astype(BF16).astype(F32)
+    bias_ref[...] = bias * LOG2E
 
     top = den = att = None
     for step, dists in ((0, (0,)), (2, (2,)), (1, (1, 3))):
@@ -369,14 +367,14 @@
             raw = nt_dot(q2[...], kb)
             for j in range(2):
                 r = rows[2 * n + j]
-                t = raw[:, j * 128 : (j + 1) * 128] * mult_ref[pl.ds(r, 1), :]
+                t = raw[:, j * 128 : (j + 1) * 128] * inv_ref[pl.ds(r, 1), :]
                 t = t + bias_ref[pl.ds(r, 1), :]
                 sc[:, (2 * n + j) * 128 : (2 * n + j + 1) * 128] = t
                 new = t if new is None else jnp.maximum(new, t)
         new = jnp.broadcast_to(jnp.max(new, axis=1, keepdims=True), (256, 128))
         if top is not None:
             new = jnp.maximum(top, new)
-            alpha = jnp.exp(top - new)
+            alpha = jnp.exp2(top - new)
             den = den * alpha
             att = att * alpha
         top = new
@@ -384,7 +382,7 @@
             ps = []
             for j in range(2):
                 r = rows[2 * n + j]
-                e = jnp.exp(sc[:, (2 * n + j) * 128 : (2 * n + j + 1) * 128] - top)
+                e = jnp.exp2(sc[:, (2 * n + j) * 128 : (2 * n + j + 1) * 128] - top)
                 den = e if den is None else den + e
                 ps.append((e * inv_ref[pl.ds(r, 1), :]).astype(BF16))
             p = jnp.concatenate(ps, axis=1)
@@ -462,7 +460,6 @@
             pltpu.VMEM((8, 1, 128), F32),
             pltpu.VMEM((16, 128), F32),
             pltpu.VMEM((16, 128), F32),
-            pltpu.VMEM((16, 128), F32),
             pltpu.VMEM((256, 1024), F32),
             dma((CHUNKS,)),
             dma((9,)),

time: 31.8 us -> 31.8 us (level)
  no operation moved by 1% of the time
where the time goes in v9:
time: 31.8 us; the launch traced here: 31.7 us
  Pallas kernels  30.4 us (96%)
  between operations  0.66 us (2%)
  local copies, waits for them, and re-layouts  0.6 us (2%)
    pallas_call x1, Pallas kernels, on_device(): pl.pallas_call(kernel, out_shape=pltpu.VMEM((8, 32), F32), in_specs=[pl.B...  30.4 us

profile of v9, /device:TPU:1, one launch (start us, length us, event | category | flops | bytes accessed | tf_op | source)
XLA Modules:
  0.0 31.7 jit_solution(7408695284518506062)
XLA Ops:
  0.7 30.4 %fused.1 = f32[8,32]{1,0:T(8,128)S(1)} custom-call(s32[1,1]{1,0:T(1,128)S(6)} %copy.12.len_hbm, f32[1,8192,128]{2,1,0:T(8,128)} %beh_hbm.1, s32[1,8192]{1,0:T(1,128)} %ids_hbm.1, s32[64,128]{1,0:T(8,128)} %bitcast.3, bf16[8,32,128]{2,1,0:T(8,128)(2,1)} %cand_hbm.1, bf16[128,128]{1,0:T(8,128)(2,1)} %wq_hbm.1, bf16[128,128]{1,0:T(8,128)(2,1)} %wk_hbm.1, ...), custom_call_target="tpu_custom_call" | custom-call | tf_op jit(solution)/shard_map/fused/pallas_call | solution.py:422
  31.1 0.6 %copy.11 = f32[8,32]{1,0:T(8,128)} copy(f32[8,32]{1,0:T(8,128)S(1)} %fused.1) | data formatting | bytes 2048
